TPU v7x, 128 devices: a whole 4x4x4 slice. The times are simulated.
128 devices in a mesh: row: 16 (over x, y_lo, core), col: 8 (over z, y_hi).
Axes of the slice: x: 4, y: 4 (y_hi: 2, y_lo: 2; y = y_hi * 2 + y_lo), z: 4, core: 2. Of those that a mesh axis runs over, the one named last changes fastest.
Arguments:
- documents: bfloat16 [2, 16384, 2048], P(None, ('row', 'col')), may hold values from -6 to 6
- targets: bfloat16 [2, 16384, 2048], P(None, ('row', 'col')), may hold values from -6 to 6
- routes: int32 [2, 16384, 1], P(None, ('row', 'col')), may hold values from 0 to 127; in each aligned block of 128 rows (0 to 127, 128 to 255, ..., all dimensions but the last counted through in order) at most 2 rows name the same one
- doc_counts: int32 [16, 8], replicated, may hold values from 1 to 64
- module_one: float32 [16, 2048, 2048], P('row', 'col'), may hold values from -6 to 6
- module_two: float32 [8, 2048, 2048], P('col', 'row'), may hold values from -6 to 6
- moment_one: float32 [16, 2048, 2048], P('row', 'col'), may hold values from -0.75 to 0.75
- moment_two: float32 [8, 2048, 2048], P('col', 'row'), may hold values from -0.75 to 0.75
Outputs:
- new_one: float32 [16, 2048, 2048], P('row', 'col')
- new_two: float32 [8, 2048, 2048], P('col', 'row')
- next_moment_one: float32 [16, 2048, 2048], P('row', 'col')
- next_moment_two: float32 [8, 2048, 2048], P('col', 'row')
Inputs may be any that keep to these rules, and one draw needn't show every extreme that they name: `routes`: in each micro-batch, at most 2 of the 128 rows that one device holds name the same path.
All inputs are finite; a program needn't handle non-finite values.
Results may differ from a plain program's by a relative error of at most 0.011.
Values may be sent and summed in bfloat16 or wider, within the bound.
A program may use at most 192 MiB of HBM per device.

v0:
```python
import jax
import jax.numpy as jnp
from jax import lax
from jax.sharding import PartitionSpec as P

D = 2048


beta_one = 0.9
beta_two = 0.95
inner_rate = 0.1
decay = 0.1
outer_rate = 0.7
outer_moment = 0.9


def in_blocks(shard, dim, count):
    before, after = (shard.shape[:dim], shard.shape[dim + 1 :])
    return jnp.moveaxis(shard.reshape(*before, count, -1, *after), dim, 0)


def joined_along(pieces, dim):
    dims = list(pieces.shape[1:])
    dims[dim] *= pieces.shape[0]
    return jnp.moveaxis(pieces, 0, dim).reshape(dims)


def one_exchange(shard, axis, axes, splits, concats):
    sizes = [lax.axis_size(a) for a in axes]
    pieces = in_blocks(shard, splits[0], sizes[0])
    pieces = jnp.moveaxis(in_blocks(pieces, splits[1] + 1, sizes[1]), 0, 1)
    inside = pieces.shape[2:]
    pieces = pieces.reshape(-1, *inside)
    pieces = lax.all_to_all(pieces, axis, split_axis=0, concat_axis=0, tiled=True)
    pieces = joined_along(pieces.reshape(*sizes, *inside), concats[0] + 1)
    return joined_along(pieces, concats[1])


def silu_slope(pre):
    sig = jax.nn.sigmoid(pre)
    return sig * (1.0 + pre * (1.0 - sig))


def gradients(w_one, w_two, rows, targs, valid, rows_dev):
    scale = D ** (-0.5)
    pre = jnp.dot(rows, w_one, preferred_element_type=jnp.float32) * scale
    hidden = jax.nn.silu(pre).astype(jnp.bfloat16)
    out = (
        rows.astype(jnp.float32)
        + jnp.dot(hidden, w_two, preferred_element_type=jnp.float32) * scale
    )
    error = ((out - targs.astype(jnp.float32)) * valid / rows_dev).astype(jnp.bfloat16)
    grad_two = (
        lax.dot_general(hidden, error, (((0,), (0,)), ((), ())), preferred_element_type=jnp.float32)
        * scale
    )
    back = (
        lax.dot_general(error, w_two, (((1,), (1,)), ((), ())), preferred_element_type=jnp.float32)
        * scale
    )
    inner = (back * silu_slope(pre)).astype(jnp.bfloat16)
    grad_one = (
        lax.dot_general(rows, inner, (((0,), (0,)), ((), ())), preferred_element_type=jnp.float32)
        * scale
    )
    return (grad_one, grad_two)


def adamw(param, grad, first, second, step, guard):
    first = beta_one * first + (1.0 - beta_one) * grad
    second = beta_two * second + (1.0 - beta_two) * grad * grad
    fix_one = 1.0 - beta_one ** (step + 1)
    fix_two = 1.0 - beta_two ** (step + 1)
    update = first / fix_one / (jnp.sqrt(second / fix_two) + guard) + decay * param
    return (param - inner_rate * update, first, second)


def rounded(value):
    return lax.optimization_barrier(value.astype(jnp.bfloat16)).astype(jnp.float32)


def shards(documents, targets, routes, doc_counts, module_one, module_two, moment_one, moment_two):
    n_row = lax.axis_size("row")
    n_col = lax.axis_size("col")
    paths = n_row * n_col
    row_id = lax.axis_index("row")
    col_id = lax.axis_index("col")
    micro, rows_dev, width = documents.shape
    room = max(2, 2 * rows_dev // paths)
    slots_all = paths * micro * room
    guard = 0.5 / (D * rows_dev) ** 0.5
    dest = routes[:, :, 0]
    hit = (dest[:, :, None] == jnp.arange(paths, dtype=jnp.int32)[None, None, :]).astype(jnp.int32)
    before = jnp.cumsum(hit, axis=1) - hit
    slot_rank = jnp.sum(before * hit, axis=2)
    micro_ids = jnp.arange(micro, dtype=jnp.int32)[:, None]
    target_slot = dest * (micro * room) + micro_ids * room + slot_rank
    place = (
        target_slot[:, :, None] == jnp.arange(slots_all, dtype=jnp.int32)[None, None, :]
    ).astype(jnp.bfloat16)
    sent_docs = jnp.einsum(
        "mrs,mrd->sd", place, documents, preferred_element_type=jnp.float32
    ).astype(jnp.bfloat16)
    sent_targs = jnp.einsum(
        "mrs,mrd->sd", place, targets, preferred_element_type=jnp.float32
    ).astype(jnp.bfloat16)
    sent_valid = jnp.sum(place, axis=(0, 1))
    got_docs, got_targs, got_valid = (
        one_exchange(
            sent_docs.reshape(n_row, n_col, micro, room, width),
            ("row", "col"),
            ("row", "col"),
            (0, 1),
            (0, 1),
        ),
        one_exchange(
            sent_targs.reshape(n_row, n_col, micro, room, width),
            ("row", "col"),
            ("row", "col"),
            (0, 1),
            (0, 1),
        ),
        one_exchange(
            sent_valid.reshape(n_row, n_col, micro, room),
            ("row", "col"),
            ("row", "col"),
            (0, 1),
            (0, 1),
        ),
    )
    got_docs = got_docs.reshape(paths, micro, room, width)
    got_targs = got_targs.reshape(paths, micro, room, width)
    got_valid = got_valid.reshape(paths, micro, room)
    start_one = lax.all_gather(module_one.astype(jnp.bfloat16), "col", axis=1, tiled=True)[0]
    start_two = lax.all_gather(module_two.astype(jnp.bfloat16), "row", axis=1, tiled=True)[0]
    p_one = start_one.astype(jnp.float32)
    p_two = start_two.astype(jnp.float32)
    m_one = jnp.zeros_like(p_one)
    v_one = jnp.zeros_like(p_one)
    m_two = jnp.zeros_like(p_two)
    v_two = jnp.zeros_like(p_two)
    for step in range(micro):
        rows = got_docs[:, step].reshape(paths * room, width)
        targs = got_targs[:, step].reshape(paths * room, width)
        valid = got_valid[:, step].reshape(paths * room, 1).astype(jnp.float32)
        grad_one, grad_two = gradients(
            p_one.astype(jnp.bfloat16), p_two.astype(jnp.bfloat16), rows, targs, valid, rows_dev
        )
        p_one, m_one, v_one = adamw(p_one, grad_one, m_one, v_one, step, guard)
        p_two, m_two, v_two = adamw(p_two, grad_two, m_two, v_two, step, guard)
    delta_one = start_one.astype(jnp.float32) - p_one
    delta_two = start_two.astype(jnp.float32) - p_two
    counts = doc_counts.astype(jnp.float32)
    row_counts = lax.dynamic_index_in_dim(counts, row_id, 0, keepdims=False)
    col_counts = lax.dynamic_index_in_dim(counts, col_id, 1, keepdims=False)
    own_count = lax.dynamic_index_in_dim(row_counts, col_id, 0, keepdims=False)
    term_one = rounded(own_count / jnp.sum(row_counts) * delta_one)
    term_two = rounded(own_count / jnp.sum(col_counts) * delta_two)
    avg_one = lax.psum_scatter(
        term_one.astype(jnp.bfloat16), "col", scatter_dimension=0, tiled=True
    ).astype(jnp.float32)
    avg_two = lax.psum_scatter(
        term_two.astype(jnp.bfloat16), "row", scatter_dimension=0, tiled=True
    ).astype(jnp.float32)
    next_moment_one = outer_moment * moment_one + avg_one[None]
    next_moment_two = outer_moment * moment_two + avg_two[None]
    new_one = module_one - outer_rate * (outer_moment * next_moment_one + avg_one[None])
    new_two = module_two - outer_rate * (outer_moment * next_moment_two + avg_two[None])
    return (new_one, new_two, next_moment_one, next_moment_two)


def solution(mesh):
    return jax.shard_map(
        shards,
        mesh=mesh,
        in_specs=(
            P(None, ("row", "col"), None),
            P(None, ("row", "col"), None),
            P(None, ("row", "col"), None),
            P(),
            P("row", "col", None),
            P("col", "row", None),
            P("row", "col", None),
            P("col", "row", None),
        ),
        out_specs=(
            P("row", "col", None),
            P("col", "row", None),
            P("row", "col", None),
            P("col", "row", None),
        ),
        check_vma=False,
    )
```

profile of v0, /device:TPU:0, one launch (start us, length us, event | category | flops | bytes accessed | tf_op | source)
XLA Modules:
  0.0 535.1 jit_solution(17000962518069156408)
XLA Ops:
  7.2 0.0 copy-start
  7.2 0.0 all-gather.3.cloned.1.call-start
  7.2 2.8 convert_element_type.110
  10.0 0.0 all-gather.3.cloned.1.call-update
  10.1 0.0 all-gather.5.cloned.1.call-start
  10.1 2.1 convert_element_type.116
  12.2 0.0 all-gather.5.cloned.1.call-update
  12.2 0.8 fusion.66
  13.0 0.2 reduce_window_sum.11
  13.2 0.9 select_reduce_fusion
  14.1 0.8 add_add_fusion
  14.8 0.2 fusion.63
  15.0 0.8 reshape_transpose_transpose_reshape_reshape_reshape.11
  15.8 11.2 %all-to-all-start.2 = ((bf16[128,1,1,2,2]{4,3,2,1,0:T(2,128)(2,1)}), bf16[128,1,1,2,2]{4,3,2,1,0:T(2,128)(2,1)S(1)}, u32[]{:S(2)}, u32[]{:S(2)}) async-start(bf16[128,1,1,2,2]{4,3,2,1,0:T(2,128)(2,1)} %bitcast.20), calls=%async_computation.2 | async-start | bytes 131072 | tf_op jit(solution)/shard_map/all_to_all | solution.py:34
  27.0 0.7 bitcast_convert_fusion
  27.7 2.7 reshape_transpose_transpose_reshape_reshape_reshape.10
  30.4 5.8 %all-to-all-done.2 = bf16[128,1,1,2,2]{4,3,2,1,0:T(2,128)(2,1)S(1)} async-done(((bf16[128,1,1,2,2]{4,3,2,1,0:T(2,128)(2,1)}), bf16[128,1,1,2,2]{4,3,2,1,0:T(2,128)(2,1)S(1)}, u32[]{:S(2)}, u32[]{:S(2)}) %all-to-all-start.2) | async-done | bytes 1056 | tf_op jit(solution)/shard_map/all_to_all | solution.py:34
  36.1 4.8 all-to-all-start.1
  41.0 3.3 bitcast_convert_fusion.1
  44.2 4.4 reshape_transpose_transpose_reshape_reshape_reshape.9
  48.6 21.5 %all-to-all-done.1 = bf16[128,1,1,2,2,2048]{5,4,3,2,1,0:T(2,128)(2,1)S(1)} async-done(((bf16[128,1,1,2,2,2048]{5,4,3,2,1,0:T(2,128)(2,1)}), bf16[128,1,1,2,2,2048]{5,4,3,2,1,0:T(2,128)(2,1)S(1)}, u32[]{:S(2)}, u32[]{:S(2)}) %all-to-all-start.1) | async-done | bytes 2097184 | tf_op jit(solution)/shard_map/all_to_all | solution.py:34
  70.2 6.9 %all-to-all-start = ((bf16[128,1,1,2,2,2048]{5,4,3,2,1,0:T(2,128)(2,1)}), bf16[128,1,1,2,2,2048]{5,4,3,2,1,0:T(2,128)(2,1)}, u32[]{:S(2)}, u32[]{:S(2)}) async-start(bf16[128,1,1,2,2,2048]{5,4,3,2,1,0:T(2,128)(2,1)} %bitcast.117), calls=%async_computation | async-start | bytes 4194304 | tf_op jit(solution)/shard_map/all_to_all | solution.py:34
  77.1 0.2 reduce-scatter.5.cloned.1.call-start
  77.4 0.6 dynamic-slice_reduce_fusion.1
  78.0 0.6 dynamic_slice.12
  79.9 0.1 reshape.71
  80.1 0.1 reshape.69
  80.2 4.2 copy.20
  84.4 22.6 %all-to-all-done = bf16[128,1,1,2,2,2048]{5,4,3,2,1,0:T(2,128)(2,1)} async-done(((bf16[128,1,1,2,2,2048]{5,4,3,2,1,0:T(2,128)(2,1)}), bf16[128,1,1,2,2,2048]{5,4,3,2,1,0:T(2,128)(2,1)}, u32[]{:S(2)}, u32[]{:S(2)}) %all-to-all-start) | async-done | bytes 2097184 | tf_op jit(solution)/shard_map/all_to_all | solution.py:34
  107.0 4.0 copy.18
  111.1 2.5 fusion.77
  113.5 1.5 reshape_squeeze.4
  115.0 2.2 reshape_squeeze.5
  117.2 4.4 slice_convert_fusion.1
  121.7 2.7 reshape.68
  124.4 3.9 reshape.70
  128.3 35.7 %all-gather.3.cloned.1.call-done = bf16[1,2048,2048]{2,1,0:T(8,128)(2,1)} async-done(((bf16[1,256,2048]{2,1,0:T(8,128)(2,1)}), bf16[1,2048,2048]{2,1,0:T(8,128)(2,1)}) %all-gather.3.cloned.1.call-update) | async-done | bytes 8388624 | tf_op jit(solution)/shard_map/all_gather | solution.py:134
  163.9 7.1 %fusion.17 = f32[256,2048]{1,0:T(8,128)} fusion(bf16[256,2048]{1,0:T(8,128)(2,1)S(1)} %reshape_squeeze.4, bf16[1,2048,2048]{2,1,0:T(8,128)(2,1)} %all-gather.3.cloned.1.call-done), kind=kOutput, calls=%fused_computation.27 | convolution fusion | flops 2148007936 | bytes 11534336 | tf_op jit(solution)/shard_map/dot_general | solution.py:46
  171.0 43.6 %all-gather.5.cloned.1.call-done = bf16[1,2048,2048]{2,1,0:T(8,128)(2,1)} async-done(((bf16[1,128,2048]{2,1,0:T(8,128)(2,1)}), bf16[1,2048,2048]{2,1,0:T(8,128)(2,1)}) %all-gather.5.cloned.1.call-update) | async-done | bytes 8388624 | tf_op jit(solution)/shard_map/all_gather | solution.py:135
  214.6 6.7 %fusion.49 = bf16[256,2048]{1,0:T(8,128)(2,1)S(1)} fusion(f32[256,2048]{1,0:T(8,128)S(1)} %reshape.68, bf16[1,2048,2048]{2,1,0:T(8,128)(2,1)} %all-gather.5.cloned.1.call-done, bf16[256,2048]{1,0:T(8,128)(2,1)S(1)} %reshape_squeeze.4, f32[256]{0:T(256)S(1)} %reshape.69, f32[256,2048]{1,0:T(8,128)} %fusion.17), kind=kOutput, calls=%fused_computation.45 | convolution fusion | flops 2153775104 | bytes 14681088 | tf_op jit(solution)/shard_map/dot_general | solution.py:50
  221.4 1.0 copy-done.14
  222.3 2.8 fusion.54
  225.1 0.0 copy-start.15
  225.1 2.4 fusion.78
  227.5 0.0 copy-start.6
  227.5 25.7 %fusion.16 = (bf16[2048,2048]{1,0:T(8,128)(2,1)}, f32[2048,2048]{1,0:T(8,128)}) fusion(bf16[1,2048,2048]{2,1,0:T(8,128)(2,1)} %all-gather.5.cloned.1.call-done, bf16[256,2048]{1,0:T(8,128)(2,1)S(1)} %copy-done.15, f32[256,2048]{1,0:T(8,128)} %fusion.17), kind=kOutput, calls=%fused_computation.24 | convolution fusion | flops 2204631040 | bytes 36700160 | tf_op jit(solution)/shard_map/dot_general | solution.py:54
  253.3 14.1 %fusion.30 = f32[256,2048]{1,0:T(8,128)S(1)} fusion(bf16[256,2048]{1,0:T(8,128)(2,1)S(1)} %copy-done.6, f32[2048,2048]{1,0:T(8,128)S(1)} %fusion.78, bf16[1,2048,2048]{2,1,0:T(8,128)(2,1)} %all-gather.3.cloned.1.call-done), kind=kOutput, calls=%fused_computation.34 | convolution fusion | flops 2202533888 | bytes 28311552 | tf_op jit(solution)/shard_map/dot_general | solution.py:46
  267.4 0.0 copy-start.12
  267.4 6.8 %fusion.52 = bf16[256,2048]{1,0:T(8,128)(2,1)S(1)} fusion(f32[256,2048]{1,0:T(8,128)S(1)} %copy-done.5, bf16[2048,2048]{1,0:T(8,128)(2,1)} %get-tuple-element.14, bf16[256,2048]{1,0:T(8,128)(2,1)S(1)} %copy-done.6, f32[256]{0:T(256)S(1)} %reshape.71, f32[256,2048]{1,0:T(8,128)S(1)} %fusion.30), kind=kOutput, calls=%fused_computation.46 | convolution fusion | flops 2153775104 | bytes 14681088 | tf_op jit(solution)/shard_map/dot_general | solution.py:50
  274.3 0.0 copy-start.16
  274.3 1.0 copy-done.16
  275.2 1.5 copy-done.17
  276.7 30.0 %fusion.7 = bf16[2048,2048]{1,0:T(8,128)(2,1)} fusion(f32[2048,2048]{1,0:T(8,128)S(1)} %copy-done.17, bf16[1,2048,2048]{2,1,0:T(8,128)(2,1)} %all-gather.5.cloned.1.call-done, f32[]{:T(128)S(6)} %div.74, bf16[256,2048]{1,0:T(8,128)(2,1)S(1)} %fusion.52, f32[256,2048]{1,0:T(8,128)S(1)} %fusion.30), kind=kOutput, calls=%fused_computation.13 | convolution fusion | flops 2280128512 | bytes 36700164 | tf_op jit(solution)/shard_map/dot_general | solution.py:54
  306.7 0.0 reduce-scatter.5.cloned.1.call-update
  306.7 0.0 reduce-scatter.3.cloned.1.call-start
  306.8 0.6 copy-done.8
  307.4 0.7 dynamic-slice_reduce_fusion
  309.4 35.3 %fusion.3 = bf16[2048,2048]{1,0:T(8,128)(2,1)} fusion(f32[2048,2048]{1,0:T(8,128)} %copy-done.2, bf16[1,2048,2048]{2,1,0:T(8,128)(2,1)} %all-gather.3.cloned.1.call-done, f32[]{:T(128)S(6)} %div.59, bf16[256,2048]{1,0:T(8,128)(2,1)S(1)} %copy-done.6, bf16[256,2048]{1,0:T(8,128)(2,1)} %copy-done.16, bf16[2048,2048]{1,0:T(8,128)(2,1)} %get-tuple-element.14, ...), kind=kOutput, calls=%fused_computation.9 | convolution fusion | flops 4430233600 | bytes 46137348 | tf_op jit(solution)/shard_map/dot_general | solution.py:63
  344.7 0.0 reduce-scatter.3.cloned.1.call-update
  344.7 0.0 copy-start.1
  344.7 58.5 %reduce-scatter.5.cloned.1.call-done = bf16[128,2048]{1,0:T(8,128)(2,1)} async-done(((bf16[2048,2048]{1,0:T(8,128)(2,1)}), bf16[128,2048]{1,0:T(8,128)(2,1)}) %reduce-scatter.5.cloned.1.call-update) | async-done | bytes 524304 | tf_op jit(solution)/shard_map/reduce_scatter | solution.py:162
  403.2 3.4 fusion.60
  406.6 117.1 %reduce-scatter.3.cloned.1.call-done = bf16[256,2048]{1,0:T(8,128)(2,1)} async-done(((bf16[2048,2048]{1,0:T(8,128)(2,1)}), bf16[256,2048]{1,0:T(8,128)(2,1)}) %reduce-scatter.3.cloned.1.call-update) | async-done | bytes 1048592 | tf_op jit(solution)/shard_map/reduce_scatter | solution.py:159
  523.7 4.6 fusion.58
  (30 shorter events, 0.1 us)
Async XLA Ops:
  7.2 19.8 %copy-start = (bf16[2,128,2048]{2,1,0:T(8,128)(2,1)S(1)}, bf16[2,128,2048]{2,1,0:T(8,128)(2,1)}, u32[]{:S(2)}) copy-start(bf16[2,128,2048]{2,1,0:T(8,128)(2,1)} %param.9) | copy-start | bytes 3145732
  7.2 156.7 %all-gather.3.cloned.1.call-start = ((), (), s32[]{:S(2)}) async-start(), calls=%async_computation.5 | async-start | bytes 9437184 | tf_op jit(solution)/shard_map/all_gather | solution.py:134
  10.1 204.5 %all-gather.5.cloned.1.call-start = ((), (), s32[]{:S(2)}) async-start(), calls=%async_computation.6 | async-start | bytes 8912896 | tf_op jit(solution)/shard_map/all_gather | solution.py:135
  15.8 20.4 %all-to-all-start.2 = ((bf16[128,1,1,2,2]{4,3,2,1,0:T(2,128)(2,1)}), bf16[128,1,1,2,2]{4,3,2,1,0:T(2,128)(2,1)S(1)}, u32[]{:S(2)}, u32[]{:S(2)}) async-start(bf16[128,1,1,2,2]{4,3,2,1,0:T(2,128)(2,1)} %bitcast.20), calls=%async_computation.2 | async-start | bytes 131072 | tf_op jit(solution)/shard_map/all_to_all | solution.py:34
  30.4 47.0 %copy-start.9 = (s32[16,8]{0,1:T(8,128)S(1)}, s32[16,8]{0,1:T(8,128)}, u32[]{:S(2)}) copy-start(s32[16,8]{0,1:T(8,128)} %param.11) | copy-start | bytes 1540
  36.1 34.0 %all-to-all-start.1 = ((bf16[128,1,1,2,2,2048]{5,4,3,2,1,0:T(2,128)(2,1)}), bf16[128,1,1,2,2,2048]{5,4,3,2,1,0:T(2,128)(2,1)S(1)}, u32[]{:S(2)}, u32[]{:S(2)}) async-start(bf16[128,1,1,2,2,2048]{5,4,3,2,1,0:T(2,128)(2,1)} %bitcast.118), calls=%async_computation.1 | async-start | bytes 4194304 | tf_op jit(solution)/shard_map/all_to_all | solution.py:34
  70.2 10.1 %copy-start.3 = (bf16[128,1,1,2,2,2048]{5,4,3,2,1,0:T(2,128)(2,1)}, bf16[128,1,1,2,2,2048]{5,4,3,2,1,0:T(2,128)(2,1)S(1)}, u32[]{:S(2)}) copy-start(bf16[128,1,1,2,2,2048]{5,4,3,2,1,0:T(2,128)(2,1)S(1)} %all-to-all-done.1) | copy-start | bytes 6291460
  70.2 36.9 %all-to-all-start = ((bf16[128,1,1,2,2,2048]{5,4,3,2,1,0:T(2,128)(2,1)}), bf16[128,1,1,2,2,2048]{5,4,3,2,1,0:T(2,128)(2,1)}, u32[]{:S(2)}, u32[]{:S(2)}) async-start(bf16[128,1,1,2,2,2048]{5,4,3,2,1,0:T(2,128)(2,1)} %bitcast.117), calls=%async_computation | async-start | bytes 4194304 | tf_op jit(solution)/shard_map/all_to_all | solution.py:34
  77.1 326.1 %reduce-scatter.5.cloned.1.call-start = ((), (), s32[]{:S(2)}) async-start(), calls=%async_computation.8 | async-start | bytes 8912896 | tf_op jit(solution)/shard_map/reduce_scatter | solution.py:162
  77.3 2.6 copy-start.7
  214.6 7.7 %copy-start.10 = (bf16[1,2048,2048]{2,1,0:T(8,128)(2,1)S(1)}, bf16[1,2048,2048]{2,1,0:T(8,128)(2,1)}, u32[]{:S(2)}) copy-start(bf16[1,2048,2048]{2,1,0:T(8,128)(2,1)} %all-gather.5.cloned.1.call-done) | copy-start | bytes 25165828
  214.6 7.7 %copy-start.11 = (f32[256,2048]{1,0:T(8,128)S(1)}, f32[256,2048]{1,0:T(8,128)}, u32[]{:S(2)}) copy-start(f32[256,2048]{1,0:T(8,128)} %fusion.17) | copy-start | bytes 6291460
  221.4 1.0 copy-start.14
  225.1 2.4 copy-start.15
  227.5 25.8 %copy-start.2 = (f32[2048,2048]{1,0:T(8,128)}, f32[2048,2048]{1,0:T(8,128)S(1)}, u32[]{:S(2)}) copy-start(f32[2048,2048]{1,0:T(8,128)S(1)} %fusion.78) | copy-start | bytes 50331652
  227.5 25.8 %copy-start.6 = (bf16[256,2048]{1,0:T(8,128)(2,1)S(1)}, bf16[256,2048]{1,0:T(8,128)(2,1)}, u32[]{:S(2)}) copy-start(bf16[256,2048]{1,0:T(8,128)(2,1)} %reshape_squeeze.5) | copy-start | bytes 3145732
  253.3 14.1 %copy-start.5 = (f32[256,2048]{1,0:T(8,128)S(1)}, f32[256,2048]{1,0:T(8,128)}, u32[]{:S(2)}) copy-start(f32[256,2048]{1,0:T(8,128)} %reshape.70) | copy-start | bytes 6291460
  267.4 6.9 %copy-start.12 = (f32[256,2048]{1,0:T(8,128)}, f32[256,2048]{1,0:T(8,128)S(1)}, u32[]{:S(2)}) copy-start(f32[256,2048]{1,0:T(8,128)S(1)} %fusion.30) | copy-start | bytes 6291460
  267.4 9.3 %copy-start.17 = (f32[2048,2048]{1,0:T(8,128)S(1)}, f32[2048,2048]{1,0:T(8,128)}, u32[]{:S(2)}) copy-start(f32[2048,2048]{1,0:T(8,128)} %get-tuple-element.15) | copy-start | bytes 50331652
  274.3 1.0 copy-start.16
  306.7 0.7 copy-start.8
  306.7 2.7 copy-start.13
  306.7 217.0 %reduce-scatter.3.cloned.1.call-start = ((), (), s32[]{:S(2)}) async-start(), calls=%async_computation.7 | async-start | bytes 9437184 | tf_op jit(solution)/shard_map/reduce_scatter | solution.py:159
  344.7 179.0 %copy-start.4 = (f32[1,256,2048]{2,1,0:T(8,128)S(1)}, f32[1,256,2048]{2,1,0:T(8,128)}, u32[]{:S(2)}) copy-start(f32[1,256,2048]{2,1,0:T(8,128)} %param.12) | copy-start | bytes 6291460
  344.7 183.6 %copy-start.1 = (bf16[2,128,2048]{2,1,0:T(8,128)(2,1)S(1)}, bf16[2,128,2048]{2,1,0:T(8,128)(2,1)}, u32[]{:S(2)}) copy-start(bf16[2,128,2048]{2,1,0:T(8,128)(2,1)} %param.9) | copy-start | bytes 3145732
Sparse Core Ops, SparseCore 0:
  10.3 153.5 all-gather.2
  165.6 48.9 all-gather.4
  306.9 96.3 reduce-scatter.4
  406.9 116.7 reduce-scatter.2
where the time goes:
time: 540 us; the launch traced here: 535 us
  waiting for transfers between devices  305 us (56%)
  matrix products  135 us (25%)
  local copies, waits for them, and re-layouts  33.7 us (6%)
  starting transfers between devices  23.2 us (4%)
  other arithmetic  21.4 us (4%)
  between operations  16.9 us (3%)
    reduce_scatter x1, waiting for transfers between devices, shards(): lax.psum_scatter(term_one.astype(jnp.bfloat16), 'col', scatter_dimension=...  117 us
    reduce_scatter x1, waiting for transfers between devices, shards(): lax.psum_scatter(term_two.astype(jnp.bfloat16), 'row', scatter_dimension=...  58.5 us
    dot_general x2, matrix products, gradients(): lax.dot_general(hidden, error, (((0,), (0,)), ((), ())), preferred_elemen...  55.8 us
    all_to_all x3, waiting for transfers between devices, one_exchange(): lax.all_to_all(pieces, axis, split_axis=0, concat_axis=0, tiled=True)  49.9 us
    all_gather x1, waiting for transfers between devices, shards(): lax.all_gather(module_two.astype(jnp.bfloat16), 'row', axis=1, tiled=True)  43.6 us
    dot_general x2, matrix products, gradients(): lax.dot_general(rows, inner, (((0,), (0,)), ((), ())), preferred_element_...  37.7 us
    all_gather x1, waiting for transfers between devices, shards(): lax.all_gather(module_one.astype(jnp.bfloat16), 'col', axis=1, tiled=True)  35.7 us
    all_to_all x3, starting transfers between devices, one_exchange(): lax.all_to_all(pieces, axis, split_axis=0, concat_axis=0, tiled=True)  22.9 us
  transfers between devices with their start and end apart: 7, of which 7 were waited for; matrix products, arithmetic and copies ran while one was open for 17% of the time, Pallas kernels for 0%

commit v1 on v0

v1 whole, which is shorter than its diff:
```python
import functools

import jax
import jax.numpy as jnp
from jax import lax
from jax.experimental import pallas as pl
from jax.experimental.pallas import tpu as pltpu
from jax.sharding import PartitionSpec as P

D = 2048
ROWS = 128
PATHS = 128
SLOTS = 256
N_ROW = 16
N_COL = 8
SCALE = D ** (-0.5)
GUARD = 0.5 / (D * ROWS) ** 0.5 / SCALE

outer_rate = 0.7
outer_moment = 0.9

BF = jnp.bfloat16
F32 = jnp.float32
MESH = pl.DeviceIdType.MESH
ANY = pl.BlockSpec(memory_space=pl.ANY)
VMEM = pl.BlockSpec(memory_space=pltpu.VMEM)


def iota(shape, dim):
    return lax.broadcasted_iota(jnp.int32, shape, dim)


def pack_kernel(dest_col, dest_row, docs, targs, out):
    block = pl.program_id(0)
    picks = []
    for m in range(2):
        row = dest_row[m : m + 1, :]
        same = jnp.where(dest_col[m] == row, 1, 0)
        earlier = jnp.where(iota((ROWS, ROWS), 0) < iota((ROWS, ROWS), 1), same, 0)
        rank = jnp.sum(earlier, axis=0, keepdims=True)
        for kind in range(2):
            slot = row * 8 + (m * 4 + kind * 2) + rank - block * 128
            picks.append(jnp.where(iota((128, ROWS), 0) == slot, 1.0, 0.0).astype(BF))
    total = jnp.dot(picks[0], docs[0], preferred_element_type=F32)
    total += jnp.dot(picks[1], targs[0], preferred_element_type=F32)
    total += jnp.dot(picks[2], docs[1], preferred_element_type=F32)
    total += jnp.dot(picks[3], targs[1], preferred_element_type=F32)
    out[...] = total.astype(BF)


def pack(routes, docs, targs):
    full = lambda *shape: pl.BlockSpec(shape, lambda i: (0,) * len(shape))
    return pl.pallas_call(
        pack_kernel,
        grid=(8,),
        out_shape=jax.ShapeDtypeStruct((PATHS * 8, D), BF),
        in_specs=[full(2, ROWS, 1), full(2, ROWS), full(2, ROWS, D), full(2, ROWS, D)],
        out_specs=pl.BlockSpec((128, D), lambda i: (i, 0)),
        name="pack",
    )(routes, routes.reshape(2, ROWS), docs, targs)


def places():
    row, col = lax.axis_index("row"), lax.axis_index("col")
    x, low, core = row // 4, (row // 2) % 2, row % 2
    z, high = col // 2, col % 2

    def device(x=x, low=low, core=core, z=z, high=high):
        return (x * 4 + low * 2 + core, z * 2 + high)

    return row, col, x, low, core, z, high, device


def towers():
    row, col, x, low, core, z, high, device = places()
    one = dict(
        place=z,
        size=256,
        partner=device(high=1 - high),
        plus=device(z=(z + 1) % 4),
        minus=device(z=(z + 3) % 4),
        rows=lambda place, j: pl.multiple_of((place * 2 + (high + j) % 2) * 256, 256),
    )
    two = dict(
        place=x,
        size=128,
        partner=device(low=1 - low),
        plus=device(x=(x + 1) % 4),
        minus=device(x=(x + 3) % 4),
        rows=lambda place, j: pl.multiple_of((place * 4 + ((low + j) % 2) * 2 + core) * 128, 128),
    )
    return one, two, device(core=1 - core)


def remote(src, dst, send, recv, device):
    copy = pltpu.make_async_remote_copy(
        src_ref=src, dst_ref=dst, send_sem=send, recv_sem=recv, device_id=device, device_id_type=MESH
    )
    return copy


def gather_kernel(own_one, own_two, slots, w_one, w_two, got, y_sem, ring_sem, fwd_sem, core_sem, local_sem, a2a_sem):
    one, two, twin = towers()
    row, col = lax.axis_index("row"), lax.axis_index("col")
    me = row * N_COL + col
    sent = []

    def start(copy):
        copy.start()
        sent.append(copy)
        return copy

    class Tower:
        pass

    ts = []
    for n, (place, own, full) in enumerate(((one, own_one, w_one), (two, own_two, w_two))):
        t = Tower()
        t.n, t.own, t.full, t.half = n, own, full, place["size"] // 2
        t.__dict__.update(place)
        ts.append(t)

    def part(t, place, j, first, count):
        return t.full.at[pl.ds(t.rows(place, j) + first, count)]

    def spread(t, j):
        half = t.half
        for way, device in ((0, t.plus), (1, t.minus)):
            for which in (0, 1) if way == 0 else (1, 0):
                dst = part(t, t.place, j, which * half, half)
                src = t.own.at[pl.ds(which * half, half)] if j == 0 else dst
                start(remote(src, dst, ring_sem.at[0, t.n, j, way, which], ring_sem.at[1, t.n, j, way, which], device))

    def arrived(t, j, way, which):
        place = (t.place + (3 if way == 0 else 1)) % 4
        ref = part(t, place, j, which * t.half, t.half)
        remote(ref, ref, ring_sem.at[0, t.n, j, way, which], ring_sem.at[1, t.n, j, way, which], t.plus).wait_recv()

    def forward(t, j, way):
        arrived(t, j, way, way)
        place = (t.place + (3 if way == 0 else 1)) % 4
        ref = part(t, place, j, way * t.half, t.half)
        start(remote(ref, ref, fwd_sem.at[0, t.n, j, way], fwd_sem.at[1, t.n, j, way], t.plus if way == 0 else t.minus))

    def forwarded(t, j, way):
        ref = part(t, (t.place + 2) % 4, j, way * t.half, t.half)
        remote(ref, ref, fwd_sem.at[0, t.n, j, way], fwd_sem.at[1, t.n, j, way], t.plus).wait_recv()

    def to_twin(step, j):
        t = ts[1]
        dst = part(t, (t.place + step) % 4, j, 0, 128)
        src = t.own if step == 0 and j == 0 else dst
        start(remote(src, dst, core_sem.at[0, step, j], core_sem.at[1, step, j], twin))

    for t in ts:
        ref = part(t, t.place, 0, 0, 2 * t.half)
        start(remote(t.own, ref, y_sem.at[0, t.n], y_sem.at[1, t.n], t.partner))
        spread(t, 0)
    to_twin(0, 0)
    locals_ = [
        pltpu.make_async_copy(t.own, part(t, t.place, 0, 0, 2 * t.half), local_sem.at[t.n]) for t in ts
    ]
    locals_.append(pltpu.make_async_copy(slots.at[me], got.at[me], local_sem.at[2]))
    for copy in locals_:
        copy.start()

    def send_slots(step, carry):
        peer = (me + step) % PATHS
        remote(slots.at[peer], got.at[me], a2a_sem.at[0], a2a_sem.at[1], (peer // N_COL, peer % N_COL)).start()
        return carry

    lax.fori_loop(1, PATHS, send_slots, 0)
    for t in ts:
        ref = part(t, t.place, 1, 0, 2 * t.half)
        remote(ref, ref, y_sem.at[0, t.n], y_sem.at[1, t.n], t.partner).wait_recv()
        spread(t, 1)
    to_twin(0, 1)
    for j in range(2):
        for t in ts:
            for way in range(2):
                forward(t, j, way)
    for j in range(2):
        for t in ts:
            arrived(t, j, 0, 1)
            arrived(t, j, 1, 0)
        to_twin(1, j)
        to_twin(3, j)
    for j in range(2):
        for t in ts:
            forwarded(t, j, 0)
            forwarded(t, j, 1)
        to_twin(2, j)
    t = ts[1]
    for step in range(4):
        for j in range(2):
            rows = ((t.place + step) % 4 * 4 + ((row // 2 + j) % 2) * 2 + 1 - row % 2) * 128
            ref = t.full.at[pl.ds(pl.multiple_of(rows, 128), 128)]
            remote(ref, ref, core_sem.at[0, step, j], core_sem.at[1, step, j], twin).wait_recv()
    for copy in locals_:
        copy.wait()
    for copy in sent:
        copy.wait_send()
    all_slots = remote(
        slots.at[pl.ds(0, PATHS - 1)], got.at[pl.ds(0, PATHS - 1)], a2a_sem.at[0], a2a_sem.at[1], twin
    )
    all_slots.wait_send()
    all_slots.wait_recv()


def gather(own_one, own_two, slots):
    sem = pltpu.SemaphoreType.DMA
    return pl.pallas_call(
        gather_kernel,
        out_shape=(
            jax.ShapeDtypeStruct((D, D), BF),
            jax.ShapeDtypeStruct((D, D), BF),
            jax.ShapeDtypeStruct((PATHS, 8, D), BF),
        ),
        in_specs=[VMEM] * 3,
        out_specs=(ANY,) * 3,
        scratch_shapes=[
            sem((2, 2)),
            sem((2, 2, 2, 2, 2)),
            sem((2, 2, 2, 2)),
            sem((2, 4, 2)),
            sem((3,)),
            sem((2,)),
        ],
        compiler_params=pltpu.CompilerParams(has_side_effects=True),
        name="gather",
    )(own_one, own_two, slots)


def compute_kernel(
    share, got, w_one, w_two, t_one, t_two, one, two, g_one, g_two, x, y, hid, err, inn, slope, x_t, h_t, sem
):
    loads = [pltpu.make_async_copy(w_one, one, sem.at[0]), pltpu.make_async_copy(w_two, two, sem.at[1])]
    for copy in loads:
        copy.start()
    o, i = iota((256, 256), 0), iota((256, 256), 1)
    pick = jnp.where(i == (o % 64) // 2 * 8 + o // 64 * 2 + o % 2, 1.0, 0.0).astype(BF)
    for b in range(4):
        rows = jnp.dot(pick, got[b * 256 : (b + 1) * 256, :], preferred_element_type=F32).astype(BF)
        for m in range(2):
            x[m, b * 64 : (b + 1) * 64, :] = rows[m * 128 : m * 128 + 64]
            y[m, b * 64 : (b + 1) * 64, :] = rows[m * 128 + 64 : m * 128 + 128]

    tile = 256

    def spans(n):
        return pl.ds(pl.multiple_of(n * tile, tile), tile)

    def passes(m, first):
        def pre_tile(n, carry):
            cols = spans(n)
            pre = jnp.dot(x[m], one[:, cols], preferred_element_type=F32) * SCALE
            sig = 1.0 / (1.0 + jnp.exp(-pre))
            hidden = (pre * sig).astype(BF)
            hid[:, cols] = hidden
            h_t[cols, :] = hidden.T
            slope[:, cols] = sig * (1.0 + pre * (1.0 - sig))
            x_t[cols, :] = x[m, :, cols].T
            return carry

        if first:
            loads[0].wait()
        lax.fori_loop(0, D // tile, pre_tile, 0)
        if first:
            loads[1].wait()

        def err_tile(n, carry):
            cols = spans(n)
            out = jnp.dot(hid[...], two[:, cols], preferred_element_type=F32) * SCALE
            out = x[m, :, cols].astype(F32) + out
            err[:, cols] = ((out - y[m, :, cols].astype(F32)) / ROWS).astype(BF)
            return carry

        lax.fori_loop(0, D // tile, err_tile, 0)

        def inn_tile(n, carry):
            cols = spans(n)
            back = lax.dot_general(err[...], two[cols, :], (((1,), (1,)), ((), ())), preferred_element_type=F32)
            inn[:, cols] = (back * SCALE * slope[:, cols]).astype(BF)
            return carry

        lax.fori_loop(0, D // tile, inn_tile, 0)

    def first_update(left, right, w, g):
        def step(n, carry):
            rows, cols = spans(n // 4), pl.ds(pl.multiple_of(n % 4 * 512, 512), 512)
            grad = jnp.dot(left[rows, :], right[:, cols], preferred_element_type=F32)
            update = grad / (jnp.abs(grad) + GUARD)
            g[rows, cols] = grad.astype(BF)
            w[rows, cols] = (0.99 * w[rows, cols].astype(F32) - 0.1 * update).astype(BF)
            return carry

        lax.fori_loop(0, 32, step, 0)

    def last_update(left, right, w, g, weight):
        part_w, part_a, part_b = weight * (1.0 / 0.99 - 0.99), weight * (0.1 / 0.99), weight * 0.1

        def step(n, carry):
            rows, cols = spans(n // 4), pl.ds(pl.multiple_of(n % 4 * 512, 512), 512)
            grad = jnp.dot(left[rows, :], right[:, cols], preferred_element_type=F32)
            before = g[rows, cols].astype(F32)
            update_a = before / (jnp.abs(before) + GUARD)
            first = (0.09 / 0.19) * before + (0.1 / 0.19) * grad
            second = (0.0475 / 0.0975) * (before * before) + (0.05 / 0.0975) * (grad * grad)
            update_b = first / (jnp.sqrt(second) + GUARD)
            g[rows, cols] = (
                part_w * w[rows, cols].astype(F32) + part_a * update_a + part_b * update_b
            ).astype(BF)
            return carry

        lax.fori_loop(0, 32, step, 0)

    passes(0, True)
    first_update(h_t, err, two, g_two)
    first_update(x_t, inn, one, g_one)
    passes(1, False)
    last_update(x_t, inn, one, g_one, share[0])
    out_one = pltpu.make_async_copy(g_one, t_one, sem.at[0])
    out_one.start()
    last_update(h_t, err, two, g_two, share[1])
    out_two = pltpu.make_async_copy(g_two, t_two, sem.at[1])
    out_two.start()
    out_one.wait()
    out_two.wait()


def compute(share, got, w_one, w_two):
    square = jax.ShapeDtypeStruct((D, D), BF)
    act = pltpu.VMEM((SLOTS, D), BF)
    return pl.pallas_call(
        compute_kernel,
        out_shape=(square, square),
        in_specs=[pl.BlockSpec(memory_space=pltpu.SMEM), VMEM, ANY, ANY],
        out_specs=(ANY, ANY),
        scratch_shapes=[pltpu.VMEM((D, D), BF)] * 4
        + [pltpu.VMEM((2, SLOTS, D), BF)] * 2
        + [act] * 3
        + [pltpu.VMEM((SLOTS, D), F32)]
        + [pltpu.VMEM((D, SLOTS), BF)] * 2
        + [pltpu.SemaphoreType.DMA((2,))],
        compiler_params=pltpu.CompilerParams(vmem_limit_bytes=60 * 2**20),
        name="compute",
    )(share, got, w_one, w_two)


def reduce_kernel(
    t_one, t_two, avg_one, avg_two,
    early_one, early_two, late_one, late_two, pair_one, pair_two, core_in, core_sum, y_out_one, y_out_two,
    early_sem, late_sem, y_sem, core_sem,
):
    one, two, twin = towers()
    row = lax.axis_index("row")
    sent = []

    def start(copy):
        copy.start()
        sent.append(copy)
        return copy

    class Tower:
        pass

    ts = []
    for n, (place, full, early, late, pair, y_out, avg) in enumerate(
        (
            (one, t_one, early_one, late_one, pair_one, y_out_one, avg_one),
            (two, core_sum, early_two, late_two, pair_two, y_out_two, avg_two),
        )
    ):
        t = Tower()
        t.n, t.full, t.early, t.late, t.pair, t.y_out, t.avg = n, full, early, late, pair, y_out, avg
        t.__dict__.update(place)
        t.half = t.size // 2
        ts.append(t)

    def at(t, step, j, first, count):
        if t.n == 0:
            return t.full.at[pl.ds(t.rows((t.place + step) % 4, j) + first, count)]
        return t.full.at[(step * 2 + j), pl.ds(first, count)]

    def twin_rows(step, j, core):
        rows = ((two["place"] + step) % 4 * 4 + ((row // 2 + j) % 2) * 2 + core) * 128
        return t_two.at[pl.ds(pl.multiple_of(rows, 128), 128)]

    order = [(2, 1), (2, 0), (1, 1), (3, 1), (1, 0), (3, 0), (0, 1), (0, 0)]
    for step, j in order:
        slot = step * 2 + j
        start(
            remote(
                twin_rows(step, j, 1 - row % 2), core_in.at[slot], core_sem.at[0, slot], core_sem.at[1, slot], twin
            )
        )

    def send_early(t, j):
        for way, device in ((0, t.plus), (1, t.minus)):
            start(
                remote(
                    at(t, 2, j, way * t.half, t.half), t.early.at[j, way],
                    early_sem.at[0, t.n, j, way], early_sem.at[1, t.n, j, way], device,
                )
            )

    def send_plain(t, j):
        for way, device in ((0, t.plus), (1, t.minus)):
            other = 1 - way
            start(
                remote(
                    at(t, 1 if way == 0 else 3, j, other * t.half, t.half), t.late.at[j, way, other],
                    late_sem.at[0, t.n, j, way, other], late_sem.at[1, t.n, j, way, other], device,
                )
            )

    def send_joined(t, j):
        for way, device in ((0, t.plus), (1, t.minus)):
            buf = t.early.at[j, way]
            remote(
                buf, buf, early_sem.at[0, t.n, j, way], early_sem.at[1, t.n, j, way], device
            ).wait_recv()
            mine = at(t, 1 if way == 0 else 3, j, way * t.half, t.half)
            buf[...] = (mine[...].astype(F32) + buf[...].astype(F32)).astype(BF)
            start(
                remote(
                    buf, t.late.at[j, way, way],
                    late_sem.at[0, t.n, j, way, way], late_sem.at[1, t.n, j, way, way], device,
                )
            )

    def total(t, j):
        for way in range(2):
            for which in range(2):
                buf = t.late.at[j, way, which]
                remote(
                    buf, buf, late_sem.at[0, t.n, j, way, which], late_sem.at[1, t.n, j, way, which], twin
                ).wait_recv()
        full = []
        for which in range(2):
            full.append(
                at(t, 0, j, which * t.half, t.half)[...].astype(F32)
                + t.late[j, 0, which].astype(F32)
                + t.late[j, 1, which].astype(F32)
            )
        return full

    t1, t2 = ts
    for j in (1, 0):
        send_early(t1, j)
    for j in (1, 0):
        send_plain(t1, j)
    for step, j in order:
        slot = step * 2 + j
        remote(
            core_in.at[slot], core_in.at[slot], core_sem.at[0, slot], core_sem.at[1, slot], twin
        ).wait_recv()
        core_sum[slot] = (twin_rows(step, j, row % 2)[...].astype(F32) + core_in[slot].astype(F32)).astype(BF)
        if (step, j) in ((2, 1), (2, 0)):
            send_early(t2, j)
    for j in (1, 0):
        send_plain(t2, j)
    for j in (1, 0):
        for t in ts:
            send_joined(t, j)
    for t in (t2, t1):
        full = total(t, 1)
        for which in range(2):
            t.y_out[which * t.half : (which + 1) * t.half] = full[which].astype(BF)
        start(remote(t.y_out, t.pair, y_sem.at[0, t.n], y_sem.at[1, t.n], t.partner))
    for t in (t2, t1):
        full = total(t, 0)
        remote(t.pair, t.pair, y_sem.at[0, t.n], y_sem.at[1, t.n], t.partner).wait_recv()
        for which in range(2):
            rows = slice(which * t.half, (which + 1) * t.half)
            t.avg[rows] = full[which] + t.pair[rows].astype(F32)
    for copy in sent:
        copy.wait_send()


def reduce(t_one, t_two):
    sem = pltpu.SemaphoreType.DMA
    v = lambda *shape: pltpu.VMEM(shape, BF)
    return pl.pallas_call(
        reduce_kernel,
        out_shape=(jax.ShapeDtypeStruct((256, D), F32), jax.ShapeDtypeStruct((128, D), F32)),
        in_specs=[VMEM, VMEM],
        out_specs=(VMEM, VMEM),
        scratch_shapes=[
            v(2, 2, 128, D),
            v(2, 2, 64, D),
            v(2, 2, 2, 128, D),
            v(2, 2, 2, 64, D),
            v(256, D),
            v(128, D),
            v(8, 128, D),
            v(8, 128, D),
            v(256, D),
            v(128, D),
            sem((2, 2, 2, 2)),
            sem((2, 2, 2, 2, 2)),
            sem((2, 2)),
            sem((2, 8)),
        ],
        compiler_params=pltpu.CompilerParams(has_side_effects=True, vmem_limit_bytes=60 * 2**20),
        name="reduce",
    )(t_one, t_two)


def shards(documents, targets, routes, doc_counts, module_one, module_two, moment_one, moment_two):
    row_id = lax.axis_index("row")
    col_id = lax.axis_index("col")
    slots = pack(routes, documents, targets)
    w_one, w_two, got = gather(
        module_one[0].astype(BF), module_two[0].astype(BF), slots.reshape(PATHS, 8, D)
    )
    counts = doc_counts.astype(F32)
    row_counts = lax.dynamic_index_in_dim(counts, row_id, 0, keepdims=False)
    col_counts = lax.dynamic_index_in_dim(counts, col_id, 1, keepdims=False)
    own_count = lax.dynamic_index_in_dim(row_counts, col_id, 0, keepdims=False)
    share = jnp.stack([own_count / jnp.sum(row_counts), own_count / jnp.sum(col_counts)])
    t_one, t_two = compute(share, got.reshape(PATHS * 8, D), w_one, w_two)
    avg_one, avg_two = reduce(t_one, t_two)
    next_moment_one = outer_moment * moment_one + avg_one[None]
    next_moment_two = outer_moment * moment_two + avg_two[None]
    new_one = module_one - outer_rate * (outer_moment * next_moment_one + avg_one[None])
    new_two = module_two - outer_rate * (outer_moment * next_moment_two + avg_two[None])
    return (new_one, new_two, next_moment_one, next_moment_two)


def solution(mesh):
    return jax.shard_map(
        shards,
        mesh=mesh,
        in_specs=(
            P(None, ("row", "col"), None),
            P(None, ("row", "col"), None),
            P(None, ("row", "col"), None),
            P(),
            P("row", "col", None),
            P("col", "row", None),
            P("row", "col", None),
            P("col", "row", None),
        ),
        out_specs=(
            P("row", "col", None),
            P("col", "row", None),
            P("row", "col", None),
            P("col", "row", None),
        ),
        check_vma=False,
    )
```

time: 540 us -> 373 us (0.69)
  Pallas kernels: 0 us -> 353 us
  waiting for transfers between devices: 305 us -> 0 us
  matrix products: 135 us -> 0 us
  local copies, waits for them, and re-layouts: 33.7 us -> 2.08 us
  starting transfers between devices: 23.2 us -> 0 us
  between operations: 16.9 us -> 3.39 us
  other arithmetic: 21.4 us -> 14.5 us
    pallas_call x0 -> x4, Pallas kernels: none -> 353 us  [the longest x1 134 us: gather(): pl.pallas_call(gather_kernel, out_shape=(jax.ShapeDtypeStruct((D, D), BF)...]
    reduce_scatter x2 -> x0, waiting for transfers between devices: 176 us -> none  [the longest x1 117 us: shards(): lax.psum_scatter(term_one.astype(jnp.bfloat16), 'col', scatter_dimension=...]
    dot_general x11 -> x0, matrix products: 135 us -> none  [the longest x2 55.8 us: gradients(): lax.dot_general(hidden, error, (((0,), (0,)), ((), ())), preferred_elemen...]
    all_gather x2 -> x0, waiting for transfers between devices: 79.3 us -> none  [the longest x1 43.6 us: shards(): lax.all_gather(module_two.astype(jnp.bfloat16), 'row', axis=1, tiled=True)]
    all_to_all x3 -> x0, waiting for transfers between devices: 49.9 us -> none  [one_exchange(): lax.all_to_all(pieces, axis, split_axis=0, concat_axis=0, tiled=True)]
    all_to_all x3 -> x0, starting transfers between devices: 22.9 us -> none  [one_exchange(): lax.all_to_all(pieces, axis, split_axis=0, concat_axis=0, tiled=True)]
    another operation x5 -> x0, local copies, waits for them, and re-layouts: 11.6 us -> none  [the longest x3 7.86 us: one_exchange(): pieces = pieces.reshape(-1, *inside)]
    transpose x3 -> x0, local copies, waits for them, and re-layouts: 8.2 us -> none  [joined_along(): return jnp.moveaxis(pieces, 0, dim).reshape(dims)]
  transfers between devices with their start and end apart: 7 -> 0, of which waited for: 7 -> 0; matrix products, arithmetic and copies ran while one was open for 17% -> 0% of each run, Pallas kernels for 0% -> 0%
where the time goes in v1:
time: 373 us
  Pallas kernels  353 us (95%)
  other arithmetic  14.5 us (4%)
    pallas_call x1, Pallas kernels, gather(): pl.pallas_call(gather_kernel, out_shape=(jax.ShapeDtypeStruct((D, D), BF)...  134 us
    pallas_call x1, Pallas kernels, reduce(): pl.pallas_call(reduce_kernel, out_shape=(jax.ShapeDtypeStruct((256, D), F...  116 us
    pallas_call x1, Pallas kernels, compute(): pl.pallas_call(compute_kernel, out_shape=(square, square), in_specs=[pl.B...  94.4 us
    pallas_call x1, Pallas kernels, pack(): pl.pallas_call(pack_kernel, grid=(8,), out_shape=jax.ShapeDtypeStruct((PA...  8.71 us

profile of v1, /device:TPU:0, one launch (start us, length us, event | category | flops | bytes accessed | tf_op | source)
XLA Modules:
  0.0 372.8 jit_solution(5922994992936614861)
XLA Ops:
  0.6 0.7 convert_element_type.13
  1.3 0.6 dynamic-slice_reduce_fusion.1
  1.9 0.7 dynamic-slice_reduce_fusion
  2.6 0.6 dynamic_slice.12
  5.9 0.6 pad_maximum_fusion.share
  6.5 1.5 copy.12.dest_col
  7.9 2.1 convert_bitcast_fusion.1.own_two
  10.0 2.7 convert_bitcast_fusion.own_one
  12.7 8.7 %pack.1 = bf16[1024,2048]{1,0:T(8,128)(2,1)} custom-call(s32[2,128,1]{2,1,0:T(8,128)} %copy.12.dest_col, s32[2,128]{1,0:T(2,128)} %bitcast.28, bf16[2,128,2048]{2,1,0:T(8,128)(2,1)} %docs.1, bf16[2,128,2048]{2,1,0:T(8,128)(2,1)} %targs.1), custom_call_target="tpu_custom_call" | custom-call | tf_op jit(solution)/shard_map/pack/pallas_call | solution.py:53
  21.4 133.8 %gather.1 = (bf16[2048,2048]{1,0:T(8,128)(2,1)}, bf16[2048,2048]{1,0:T(8,128)(2,1)}, bf16[128,8,2048]{2,1,0:T(8,128)(2,1)}) custom-call(bf16[256,2048]{1,0:T(8,128)(2,1)} %convert_bitcast_fusion.own_one, bf16[128,2048]{1,0:T(8,128)(2,1)} %convert_bitcast_fusion.1.own_two, bf16[128,8,2048]{2,1,0:T(8,128)(2,1)} %bitcast.26), custom_call_target="tpu_custom_call" | custom-call | tf_op jit(solution)/shard_map/gather/pallas_call | solution.py:212
  155.2 94.4 %compute.1 = (bf16[2048,2048]{1,0:T(8,128)(2,1)}, bf16[2048,2048]{1,0:T(8,128)(2,1)}) custom-call(f32[2]{0:T(128)} %pad_maximum_fusion.share, bf16[1024,2048]{1,0:T(8,128)(2,1)} %bitcast.27, bf16[2048,2048]{1,0:T(8,128)(2,1)} %get-tuple-element.12.w_one, bf16[2048,2048]{1,0:T(8,128)(2,1)} %get-tuple-element.13.w_two), custom_call_target="tpu_custom_call" | custom-call | tf_op jit(solution)/shard_map/compute/pallas_call | solution.py:334
  249.6 0.0 copy-start
  249.6 115.9 %reduce.3 = (f32[256,2048]{1,0:T(8,128)}, f32[128,2048]{1,0:T(8,128)}) custom-call(bf16[2048,2048]{1,0:T(8,128)(2,1)} %get-tuple-element.14.t_one, bf16[2048,2048]{1,0:T(8,128)(2,1)} %get-tuple-element.15.t_two), custom_call_target="tpu_custom_call" | custom-call | tf_op jit(solution)/shard_map/reduce/pallas_call | solution.py:484
  365.6 0.0 copy-done
  365.6 0.0 copy-start.1
  365.6 0.0 copy-start.2
  365.6 0.0 copy-start.3
  365.6 5.5 %fusion.1 = (f32[1,256,2048]{2,1,0:T(8,128)}, f32[1,256,2048]{2,1,0:T(8,128)}) fusion(f32[1,256,2048]{2,1,0:T(8,128)S(1)} %copy-done, f32[256,2048]{1,0:T(8,128)} %get-tuple-element.16, f32[1,256,2048]{2,1,0:T(8,128)} %param.14), kind=kLoop, calls=%fused_computation.3 | loop fusion | flops 3145728 | bytes 10485760 | tf_op jit(solution)/shard_map/sub | solution.py:526
  371.1 0.0 copy-done.1
  371.1 0.0 copy-done.2
  371.1 0.0 copy-done.3
  371.1 1.7 fusion.3
Async XLA Ops:
  249.6 116.0 %copy-start = (f32[1,256,2048]{2,1,0:T(8,128)S(1)}, f32[1,256,2048]{2,1,0:T(8,128)}, u32[]{:S(2)}) copy-start(f32[1,256,2048]{2,1,0:T(8,128)} %param.12) | copy-start | bytes 6291460
  365.6 5.5 %copy-start.1 = (f32[1,128,2048]{2,1,0:T(8,128)S(1)}, f32[1,128,2048]{2,1,0:T(8,128)}, u32[]{:S(2)}) copy-start(f32[1,128,2048]{2,1,0:T(8,128)} %param.13) | copy-start | bytes 3145732
  365.6 5.5 %copy-start.2 = (f32[1,128,2048]{2,1,0:T(8,128)S(1)}, f32[1,128,2048]{2,1,0:T(8,128)}, u32[]{:S(2)}) copy-start(f32[1,128,2048]{2,1,0:T(8,128)} %param.15) | copy-start | bytes 3145732
  365.6 5.5 %copy-start.3 = (f32[128,2048]{1,0:T(8,128)S(1)}, f32[128,2048]{1,0:T(8,128)}, u32[]{:S(2)}) copy-start(f32[128,2048]{1,0:T(8,128)} %get-tuple-element.17) | copy-start | bytes 3145732

commit v2 on v0

v2 whole, which is shorter than its diff:
```python
import functools

import jax
import jax.numpy as jnp
from jax import lax
from jax.experimental import pallas as pl
from jax.experimental.pallas import tpu as pltpu
from jax.sharding import PartitionSpec as P

D = 2048
ROWS = 128
PATHS = 128
SLOTS = 256
N_ROW = 16
N_COL = 8
SCALE = D ** (-0.5)
GUARD = 0.5 / (D * ROWS) ** 0.5 / SCALE

outer_rate = 0.7
outer_moment = 0.9

BF = jnp.bfloat16
F32 = jnp.float32
MESH = pl.DeviceIdType.MESH
ANY = pl.BlockSpec(memory_space=pl.ANY)
VMEM = pl.BlockSpec(memory_space=pltpu.VMEM)


def iota(shape, dim):
    return lax.broadcasted_iota(jnp.int32, shape, dim)


def pack_kernel(dest_col, dest_row, docs, targs, out):
    block = pl.program_id(0) % 4
    row = dest_row[0]
    same = jnp.where(dest_col[0] == row, 1, 0)
    earlier = jnp.where(iota((ROWS, ROWS), 0) < iota((ROWS, ROWS), 1), same, 0)
    rank = jnp.sum(earlier, axis=0, keepdims=True)
    total = jnp.zeros((256, D // 2), F32)
    for kind, source in enumerate((docs, targs)):
        for half in range(2):
            slot = row * 8 + (kind * 4 + half) + rank * 2 - block * 256
            pick = jnp.where(iota((256, ROWS), 0) == slot, 1.0, 0.0).astype(BF)
            total += jnp.dot(pick, source[0, :, half * 1024 : (half + 1) * 1024], preferred_element_type=F32)
    out[...] = total.astype(BF)


def pack(routes, docs, targs):
    return pl.pallas_call(
        pack_kernel,
        grid=(8,),
        out_shape=jax.ShapeDtypeStruct((2 * PATHS * 8, D // 2), BF),
        in_specs=[
            pl.BlockSpec((1, ROWS, 1), lambda i: (i // 4, 0, 0)),
            pl.BlockSpec((1, 1, ROWS), lambda i: (i // 4, 0, 0)),
            pl.BlockSpec((1, ROWS, D), lambda i: (i // 4, 0, 0)),
            pl.BlockSpec((1, ROWS, D), lambda i: (i // 4, 0, 0)),
        ],
        out_specs=pl.BlockSpec((256, D // 2), lambda i: (i, 0)),
        name="pack",
    )(routes, routes.reshape(2, 1, ROWS), docs, targs)


P_ROWS = 160
Q_ROWS = 256 - P_ROWS


class Stream:
    def __init__(self, **fields):
        self.__dict__.update(fields)

    def at(self, full, step, first, count):
        return full.at[pl.ds(pl.multiple_of(self.rows((self.place + step) % 4), 16) + first, count)]


def remote(src, dst, sems, device):
    return pltpu.make_async_remote_copy(
        src_ref=src, dst_ref=dst, send_sem=sems.at[0], recv_sem=sems.at[1], device_id=device, device_id_type=MESH
    )


def round_kernel(
    counts, own_one, own_two, slots, got, avg_one, avg_two,
    one, two, g_one, g_two, stage, x, y, hid, err, inn, slope, x_t, h_t,
    early_p, late_p, pair_p, y_q, early_q, late_q, core_in, early_t, late_t, pair_t,
    ring_sem, fwd_sem, y_sem, q_sem, core_sem, a2a_sem, local_sem,
    early_sem, late_sem, pair_sem, yq_sem, core_two_sem,
):
    row, col = lax.axis_index("row"), lax.axis_index("col")
    xx, low, core = row // 4, (row // 2) % 2, row % 2
    z, high = col // 2, col % 2
    me = row * N_COL + col

    def device(x=xx, low=low, core=core, z=z, high=high):
        return (x * 4 + low * 2 + core, z * 2 + high)

    twin = device(core=1 - core)
    ring_one = dict(place=z, plus=device(z=(z + 1) % 4), minus=device(z=(z + 3) % 4), partner=device(high=1 - high))
    ring_two = dict(place=xx, plus=device(x=(xx + 1) % 4), minus=device(x=(xx + 3) % 4), partner=device(low=1 - low))

    def rows_one(first, j):
        return lambda place: (place * 2 + (high + j) % 2) * 256 + first

    def rows_two(j, core=core):
        return lambda place: (place * 4 + ((low + j) % 2) * 2 + core) * 128

    p0 = Stream(n=0, half=P_ROWS // 2, rows=rows_one(0, 0), **ring_one)
    p1 = Stream(n=1, half=P_ROWS // 2, rows=rows_one(0, 1), **ring_one)
    q0 = Stream(n=2, half=Q_ROWS // 2, rows=rows_one(P_ROWS, 0), **ring_one)
    q1 = Stream(half=Q_ROWS // 2, rows=rows_one(P_ROWS, 1), **ring_one)
    t0 = Stream(n=3, half=64, rows=rows_two(0), **ring_two)
    t1 = Stream(n=4, half=64, rows=rows_two(1), **ring_two)
    u0 = Stream(half=64, rows=rows_two(0, 1 - core), **ring_two)
    u1 = Stream(half=64, rows=rows_two(1, 1 - core), **ring_two)
    sent = []

    def start(copy):
        copy.start()
        sent.append(copy)

    def whole(s, full, step):
        return s.at(full, step, 0, 2 * s.half)

    def spread(s, full, own=None):
        for way, to in ((0, s.plus), (1, s.minus)):
            for which in (0, 1) if way == 0 else (1, 0):
                dst = s.at(full, 0, which * s.half, s.half)
                src = dst if own is None else own.at[pl.ds(which * s.half, s.half)]
                start(remote(src, dst, ring_sem.at[s.n, way, which], to))

    def arrived(s, full, way, which):
        ref = s.at(full, 3 if way == 0 else 1, which * s.half, s.half)
        remote(ref, ref, ring_sem.at[s.n, way, which], twin).wait_recv()

    def forward(s, full):
        for way, to in ((0, s.plus), (1, s.minus)):
            arrived(s, full, way, way)
            ref = s.at(full, 3 if way == 0 else 1, way * s.half, s.half)
            start(remote(ref, ref, fwd_sem.at[s.n, way], to))

    def rest(s, full):
        arrived(s, full, 0, 1)
        arrived(s, full, 1, 0)

    def forwarded(s, full):
        for way in range(2):
            ref = s.at(full, 2, way * s.half, s.half)
            remote(ref, ref, fwd_sem.at[s.n, way], twin).wait_recv()

    def q_across(step, src=None):
        dst = whole(q0, one, step)
        start(remote(dst if src is None else src, dst, q_sem.at[step], q0.partner))

    def to_twin(s, j, step, src=None):
        dst = whole(s, two, step)
        start(remote(dst if src is None else src, dst, core_sem.at[step, j], twin))

    own_p, own_q = own_one.at[pl.ds(0, P_ROWS)], own_one.at[pl.ds(P_ROWS, Q_ROWS)]
    start(remote(own_p, whole(p0, one, 0), y_sem.at[0], p0.partner))
    start(remote(own_two, whole(t0, two, 0), y_sem.at[1], t0.partner))
    spread(p0, one, own_p)
    spread(t0, two, own_two)
    spread(q0, one, own_q)
    q_across(0, own_q)
    to_twin(t0, 0, 0, own_two)
    locals_ = [
        pltpu.make_async_copy(own_p, whole(p0, one, 0), local_sem.at[0]),
        pltpu.make_async_copy(own_q, whole(q0, one, 0), local_sem.at[1]),
        pltpu.make_async_copy(own_two, whole(t0, two, 0), local_sem.at[2]),
        pltpu.make_async_copy(slots.at[0, me], got.at[0, me], local_sem.at[3]),
        pltpu.make_async_copy(slots.at[1, me], got.at[1, me], local_sem.at[4]),
    ]
    for copy in locals_:
        copy.start()

    def send_slots(m):
        def send(step, carry):
            t = step * 53 % PATHS
            to = device(
                x=(xx + t % 4) % 4,
                low=(low + t // 4 % 2) % 2,
                high=(high + t // 8 % 2) % 2,
                z=(z + t // 16 % 4) % 4,
                core=(core + t // 64) % 2,
            )
            remote(slots.at[m, to[0] * N_COL + to[1]], got.at[m, me], a2a_sem.at[m], to).start()
            return carry

        lax.fori_loop(1, PATHS, send, 0)

    def all_slots(m):
        return remote(slots.at[m, pl.ds(0, PATHS - 1)], got.at[m, pl.ds(0, PATHS - 1)], a2a_sem.at[m], twin)

    send_slots(0)
    remote(own_p, whole(p1, one, 0), y_sem.at[0], twin).wait_recv()
    spread(p1, one)
    remote(own_two, whole(t1, two, 0), y_sem.at[1], twin).wait_recv()
    spread(t1, two)
    to_twin(t1, 1, 0)
    forward(p0, one)
    forward(t0, two)
    forward(q0, one)
    forward(p1, one)
    forward(t1, two)
    rest(q0, one)
    q_across(1)
    q_across(3)
    for j, s in ((0, t0), (1, t1)):
        rest(s, two)
        to_twin(s, j, 1)
        to_twin(s, j, 3)
    forwarded(q0, one)
    q_across(2)
    for j, s in ((0, t0), (1, t1)):
        forwarded(s, two)
        to_twin(s, j, 2)
    send_slots(1)
    for step in range(4):
        ref = whole(q1, one, step)
        remote(ref, ref, q_sem.at[step], twin).wait_recv()
        for j, s in ((0, u0), (1, u1)):
            ref = whole(s, two, step)
            remote(ref, ref, core_sem.at[step, j], twin).wait_recv()
    for s in (p0, p1):
        rest(s, one)
        forwarded(s, one)
    for copy in locals_:
        copy.wait()
    all_slots(0).wait_recv()

    def unpack(m):
        o, i = iota((256, 256), 0), iota((256, 256), 1)
        source = o % 64 // 2 * 8 + o // 128 * 4 + o % 2 * 2 + o // 64 % 2
        pick = jnp.where(i == source, 1.0, 0.0).astype(BF)
        loads = [
            pltpu.make_async_copy(got.at[m, pl.ds(b * 32, 32)], stage.at[b % 2], local_sem.at[5 + b % 2]) for b in range(4)
        ]
        loads[0].start()
        loads[1].start()
        for b in range(4):
            loads[b].wait()
            part = stage[b % 2].reshape(256, D // 2)
            rows = jnp.dot(pick, part, preferred_element_type=F32).astype(BF)
            for half in range(2):
                cols = slice(half * 1024, (half + 1) * 1024)
                x[b * 64 : (b + 1) * 64, cols] = rows[half * 64 : half * 64 + 64]
                y[b * 64 : (b + 1) * 64, cols] = rows[128 + half * 64 : 192 + half * 64]
            if b < 2:
                loads[b + 2].start()

    def spans(n, tile):
        return pl.ds(pl.multiple_of(n * tile, tile), tile)

    def passes():
        wide = 1024

        def pre_tile(n, carry):
            cols = spans(n, wide)
            pre = jnp.dot(x[...], one[:, cols], preferred_element_type=F32) * SCALE
            sig = 1.0 / (1.0 + jnp.exp(-pre))
            hid[:, cols] = (pre * sig).astype(BF)
            slope[:, cols] = sig * (1.0 + pre * (1.0 - sig))
            return carry

        lax.fori_loop(0, D // wide, pre_tile, 0)

        def err_tile(n, carry):
            cols = spans(n, wide)
            out = jnp.dot(hid[...], two[:, cols], preferred_element_type=F32) * SCALE
            out = x[:, cols].astype(F32) + out
            err[:, cols] = ((out - y[:, cols].astype(F32)) / ROWS).astype(BF)
            return carry

        lax.fori_loop(0, D // wide, err_tile, 0)

        def inn_tile(n, carry):
            cols = spans(n, wide)
            back = lax.dot_general(err[...], two[cols, :], (((1,), (1,)), ((), ())), preferred_element_type=F32)
            inn[:, cols] = (back * SCALE * slope[:, cols]).astype(BF)
            return carry

        lax.fori_loop(0, D // wide, inn_tile, 0)

        def turn(n, carry):
            cols = spans(n, 256)
            x_t[cols, :] = x[:, cols].T
            h_t[cols, :] = hid[:, cols].T
            return carry

        lax.fori_loop(0, D // 256, turn, 0)

    def first_update(left, right, w, g):
        def step(n, carry):
            rows, cols = spans(n // 4, 1024), spans(n % 4, 512)
            grad = jnp.dot(left[rows, :], right[:, cols], preferred_element_type=F32)
            update = grad / (jnp.abs(grad) + GUARD)
            g[rows, cols] = grad.astype(BF)
            w[rows, cols] = (0.99 * w[rows, cols].astype(F32) - 0.1 * update).astype(BF)
            return carry

        lax.fori_loop(0, 8, step, 0)

    tally = counts[...].astype(F32)
    in_row = jnp.where(iota((N_ROW, N_COL), 0) == row, tally, 0.0)
    in_col = jnp.where(iota((N_ROW, N_COL), 1) == col, tally, 0.0)
    mine = jnp.where(iota((N_ROW, N_COL), 1) == col, in_row, 0.0)

    def grand(v):
        return jnp.sum(jnp.sum(v, axis=0, keepdims=True), axis=1, keepdims=True)

    share_one, share_two = grand(mine) / grand(in_row), grand(mine) / grand(in_col)
    root = (0.05 / 0.0975) ** 0.5

    def last_update(left, right, w, g, weight, first_row):
        part_w, part_a = weight * (1.0 / 0.99 - 0.99), weight * (0.1 / 0.99)
        part_b = weight * (0.1 * (0.1 / 0.19) / root)

        def step(n, carry):
            rows, cols = pl.ds(pl.multiple_of(first_row, 512), 512), spans(n, 512)
            grad = jnp.dot(left[rows, :], right[:, cols], preferred_element_type=F32)
            before = g[rows, cols].astype(F32)
            update_a = before / (jnp.abs(before) + GUARD)
            second = 0.95 * (before * before) + grad * grad
            update_b = (0.9 * before + grad) / (jnp.sqrt(second) + GUARD / root)
            g[rows, cols] = (
                part_w * w[rows, cols].astype(F32) + part_a * update_a + part_b * update_b
            ).astype(BF)
            return carry

        lax.fori_loop(0, 4, step, 0)

    unpack(0)
    passes()
    for copy in sent:
        copy.wait_send()
    sent.clear()
    first_update(h_t, err, two, g_two)
    first_update(x_t, inn, one, g_one)
    all_slots(1).wait_recv()
    unpack(1)
    passes()

    for s, full, early, late in (
        (p0, g_one, early_p.at[0], late_p.at[0]),
        (p1, g_one, early_p.at[1], late_p.at[1]),
        (q0, g_one, early_q, late_q),
        (t0, g_two, early_t.at[0], late_t.at[0]),
        (t1, g_two, early_t.at[1], late_t.at[1]),
    ):
        s.full, s.early, s.late = full, early, late

    def send_early(s):
        for way, to in ((0, s.plus), (1, s.minus)):
            src = s.at(s.full, 2, way * s.half, s.half)
            start(remote(src, s.early.at[way], early_sem.at[s.n, way], to))

    def send_plain(s, way):
        other = 1 - way
        src = s.at(s.full, 1 if way == 0 else 3, other * s.half, s.half)
        to = s.plus if way == 0 else s.minus
        start(remote(src, s.late.at[way, other], late_sem.at[s.n, way, other], to))

    def send_joined(s):
        for way, to in ((0, s.plus), (1, s.minus)):
            buf = s.early.at[way]
            remote(buf, buf, early_sem.at[s.n, way], twin).wait_recv()
            mine = s.at(s.full, 1 if way == 0 else 3, way * s.half, s.half)
            buf[...] = (mine[...].astype(F32) + buf[...].astype(F32)).astype(BF)
            start(remote(buf, s.late.at[way, way], late_sem.at[s.n, way, way], to))

    def total(s, which):
        for way in range(2):
            buf = s.late.at[way, which]
            remote(buf, buf, late_sem.at[s.n, way, which], twin).wait_recv()
        return (
            s.at(s.full, 0, which * s.half, s.half)[...].astype(F32)
            + s.late.at[0, which][...].astype(F32)
            + s.late.at[1, which][...].astype(F32)
        )

    def join_q(step):
        buf = y_q.at[step]
        remote(buf, buf, yq_sem.at[step], twin).wait_recv()
        mine = whole(q0, g_one, step)
        mine[...] = (mine[...].astype(F32) + buf[...].astype(F32)).astype(BF)

    def join_core(s, j, step):
        buf = core_in.at[step, j]
        remote(buf, buf, core_two_sem.at[step, j], twin).wait_recv()
        mine = whole(s, g_two, step)
        mine[...] = (mine[...].astype(F32) + buf[...].astype(F32)).astype(BF)

    def unit_one(step):
        last_update(x_t, inn, one, g_one, share_one, (z + step) % 4 * 512)
        start(remote(whole(q1, g_one, step), y_q.at[step], yq_sem.at[step], q1.partner))
        for s in (p1, p0):
            if step == 2:
                send_early(s)
            elif step:
                send_plain(s, step // 2)

    def unit_two(step):
        last_update(h_t, err, two, g_two, share_two, (xx + step) % 4 * 512)
        for j, s in ((1, u1), (0, u0)):
            start(remote(whole(s, g_two, step), core_in.at[step, j], core_two_sem.at[step, j], twin))

    for step in (2, 1, 3, 0):
        unit_one(step)
    unit_two(2)
    join_q(2)
    send_early(q0)
    join_q(1)
    send_plain(q0, 0)
    join_q(3)
    send_plain(q0, 1)
    for s in (p1, p0):
        send_joined(s)
    for j, s in ((1, t1), (0, t0)):
        join_core(s, j, 2)
        send_early(s)
    unit_two(1)
    for j, s in ((1, t1), (0, t0)):
        join_core(s, j, 1)
        send_plain(s, 0)
    unit_two(3)
    for j, s in ((1, t1), (0, t0)):
        join_core(s, j, 3)
        send_plain(s, 1)
    send_joined(q0)
    unit_two(0)
    join_q(0)
    for j, s in ((1, t1), (0, t0)):
        join_core(s, j, 0)
        send_joined(s)
    out_t, out_p = y.at[pl.ds(0, 128)], x.at[pl.ds(0, P_ROWS)]
    for s, out, pair, n in ((t1, out_t, pair_t, 1), (p1, out_p, pair_p, 0)):
        for which in range(2):
            out[which * s.half : (which + 1) * s.half] = total(s, which).astype(BF)
        start(remote(out, pair, pair_sem.at[n], s.partner))
    for which in range(2):
        first = P_ROWS + which * q0.half
        slope[first : first + q0.half] = total(q0, which)
    done = pltpu.make_async_copy(slope.at[pl.ds(0, 128)], avg_two, local_sem.at[5])
    for s, out, pair, n in ((t0, out_t, pair_t, 1), (p0, out_p, pair_p, 0)):
        full = [total(s, which) for which in range(2)]
        remote(out, pair, pair_sem.at[n], twin).wait_recv()
        if n == 0:
            done.wait()
        for which in range(2):
            rows = slice(which * s.half, (which + 1) * s.half)
            slope[rows] = full[which] + pair[rows].astype(F32)
        if n == 1:
            done.start()
    done = pltpu.make_async_copy(slope, avg_one, local_sem.at[5])
    done.start()
    for copy in sent:
        copy.wait_send()
    for m in range(2):
        all_slots(m).wait_send()
    done.wait()


def one_round(counts, own_one, own_two, slots):
    sem = pltpu.SemaphoreType.DMA
    v = lambda *shape: pltpu.VMEM(shape, BF)
    act = v(SLOTS, D)
    p, q = P_ROWS // 2, Q_ROWS // 2
    return pl.pallas_call(
        round_kernel,
        out_shape=(
            jax.ShapeDtypeStruct((2, PATHS, 8, D // 2), BF),
            jax.ShapeDtypeStruct((256, D), F32),
            jax.ShapeDtypeStruct((128, D), F32),
        ),
        in_specs=[VMEM, ANY, ANY, ANY],
        out_specs=(ANY, ANY, ANY),
        scratch_shapes=[v(D, D)] * 4
        + [v(2, 32, 8, D // 2)]
        + [act] * 5
        + [pltpu.VMEM((SLOTS, D), F32)]
        + [v(D, SLOTS)] * 2
        + [v(2, 2, p, D), v(2, 2, 2, p, D), v(2 * p, D)]
        + [v(4, 2 * q, D), v(2, q, D), v(2, 2, q, D)]
        + [v(4, 2, 128, D), v(2, 2, 64, D), v(2, 2, 2, 64, D), v(128, D)]
        + [sem((5, 2, 2, 2)), sem((5, 2, 2)), sem((2, 2)), sem((4, 2)), sem((4, 2, 2)), sem((2, 2)), sem((7,))]
        + [sem((5, 2, 2)), sem((5, 2, 2, 2)), sem((2, 2)), sem((4, 2)), sem((4, 2, 2))],
        compiler_params=pltpu.CompilerParams(has_side_effects=True, vmem_limit_bytes=67043328),
        name="round",
    )(counts, own_one, own_two, slots)


def shards(documents, targets, routes, doc_counts, module_one, module_two, moment_one, moment_two):
    slots = pack(routes, documents, targets)
    got, avg_one, avg_two = one_round(
        doc_counts, module_one[0].astype(BF), module_two[0].astype(BF), slots.reshape(2, PATHS, 8, D // 2)
    )
    next_moment_one = outer_moment * moment_one + avg_one[None]
    next_moment_two = outer_moment * moment_two + avg_two[None]
    new_one = module_one - outer_rate * (outer_moment * next_moment_one + avg_one[None])
    new_two = module_two - outer_rate * (outer_moment * next_moment_two + avg_two[None])
    return (new_one, new_two, next_moment_one, next_moment_two)


def solution(mesh):
    return jax.shard_map(
        shards,
        mesh=mesh,
        in_specs=(
            P(None, ("row", "col"), None),
            P(None, ("row", "col"), None),
            P(None, ("row", "col"), None),
            P(),
            P("row", "col", None),
            P("col", "row", None),
            P("row", "col", None),
            P("col", "row", None),
        ),
        out_specs=(
            P("row", "col", None),
            P("col", "row", None),
            P("row", "col", None),
            P("col", "row", None),
        ),
        check_vma=False,
    )
```

time: 540 us -> 273 us (0.51)
  waiting for transfers between devices: 305 us -> 0 us
  Pallas kernels: 0 us -> 257 us
  matrix products: 135 us -> 0 us
  local copies, waits for them, and re-layouts: 33.7 us -> 2.84 us
  starting transfers between devices: 23.2 us -> 0 us
  between operations: 16.9 us -> 0.67 us
  other arithmetic: 21.4 us -> 12.6 us
    pallas_call x0 -> x2, Pallas kernels: none -> 257 us  [the longest x1 248 us: one_round(): pl.pallas_call(round_kernel, out_shape=(jax.ShapeDtypeStruct((2, PATHS, 8...]
    reduce_scatter x2 -> x0, waiting for transfers between devices: 176 us -> none  [the longest x1 117 us: shards(): lax.psum_scatter(term_one.astype(jnp.bfloat16), 'col', scatter_dimension=...]
    dot_general x11 -> x0, matrix products: 135 us -> none  [the longest x2 55.8 us: gradients(): lax.dot_general(hidden, error, (((0,), (0,)), ((), ())), preferred_elemen...]
    all_gather x2 -> x0, waiting for transfers between devices: 79.3 us -> none  [the longest x1 43.6 us: shards(): lax.all_gather(module_two.astype(jnp.bfloat16), 'row', axis=1, tiled=True)]
    all_to_all x3 -> x0, waiting for transfers between devices: 49.9 us -> none  [one_exchange(): lax.all_to_all(pieces, axis, split_axis=0, concat_axis=0, tiled=True)]
    all_to_all x3 -> x0, starting transfers between devices: 22.9 us -> none  [one_exchange(): lax.all_to_all(pieces, axis, split_axis=0, concat_axis=0, tiled=True)]
    another operation x5 -> x0, local copies, waits for them, and re-layouts: 11.6 us -> none  [the longest x3 7.86 us: one_exchange(): pieces = pieces.reshape(-1, *inside)]
    transpose x3 -> x0, local copies, waits for them, and re-layouts: 8.2 us -> none  [joined_along(): return jnp.moveaxis(pieces, 0, dim).reshape(dims)]
  transfers between devices with their start and end apart: 7 -> 0, of which waited for: 7 -> 0; matrix products, arithmetic and copies ran while one was open for 17% -> 0% of each run, Pallas kernels for 0% -> 0%
where the time goes in v2:
time: 273 us
  Pallas kernels  257 us (94%)
  other arithmetic  12.6 us (5%)
  local copies, waits for them, and re-layouts  2.84 us (1%)
    pallas_call x1, Pallas kernels, one_round(): pl.pallas_call(round_kernel, out_shape=(jax.ShapeDtypeStruct((2, PATHS, 8...  248 us
    pallas_call x1, Pallas kernels, pack(): pl.pallas_call(pack_kernel, grid=(8,), out_shape=jax.ShapeDtypeStruct((2...  9.15 us
    sub x1, other arithmetic, shards(): module_one - outer_rate * (outer_moment * next_moment_one + avg_one[None])  6.09 us

profile of v2, /device:TPU:0, one launch (start us, length us, event | category | flops | bytes accessed | tf_op | source)
XLA Modules:
  0.0 273.1 jit_solution(12671754153204859365)
XLA Ops:
  0.6 1.4 copy.13.counts
  2.0 1.5 copy.12.dest_col
  3.5 2.1 convert_bitcast_fusion.1.own_two
  5.5 2.7 convert_bitcast_fusion.own_one
  8.3 9.1 %pack.1 = bf16[2048,1024]{1,0:T(8,128)(2,1)} custom-call(s32[2,128,1]{2,1,0:T(8,128)} %copy.12.dest_col, s32[2,1,128]{2,1,0:T(1,128)} %bitcast.23, bf16[2,128,2048]{2,1,0:T(8,128)(2,1)} %docs.1, bf16[2,128,2048]{2,1,0:T(8,128)(2,1)} %targs.1), custom_call_target="tpu_custom_call" | custom-call | tf_op jit(solution)/shard_map/pack/pallas_call | solution.py:49
  17.4 247.8 %round.1 = (bf16[2,128,8,1024]{3,2,1,0:T(8,128)(2,1)}, f32[256,2048]{1,0:T(8,128)}, f32[128,2048]{1,0:T(8,128)}) custom-call(s32[16,8]{1,0:T(8,128)} %copy.13.counts, bf16[256,2048]{1,0:T(8,128)(2,1)} %convert_bitcast_fusion.own_one, bf16[128,2048]{1,0:T(8,128)(2,1)} %convert_bitcast_fusion.1.own_two, bf16[2,128,8,1024]{3,2,1,0:T(8,128)(2,1)} %bitcast.22), custom_call_target="tpu_custom_call" | custom-call | tf_op jit(solution)/shard_map/round/pallas_call | solution.py:468
  265.3 0.0 copy-start
  265.3 0.0 copy-start.1
  265.3 0.0 copy-start.2
  265.3 6.1 %fusion.1 = (f32[1,256,2048]{2,1,0:T(8,128)}, f32[1,256,2048]{2,1,0:T(8,128)}) fusion(f32[1,256,2048]{2,1,0:T(8,128)} %param.12, f32[256,2048]{1,0:T(8,128)} %get-tuple-element.6, f32[1,256,2048]{2,1,0:T(8,128)} %param.14), kind=kLoop, calls=%fused_computation.3 | loop fusion | flops 3145728 | bytes 10485760 | tf_op jit(solution)/shard_map/sub | solution.py:499
  271.4 0.0 copy-done
  271.4 0.0 copy-done.1
  271.4 0.0 copy-done.2
  271.4 1.7 fusion.3
Async XLA Ops:
  265.3 6.1 %copy-start = (f32[1,128,2048]{2,1,0:T(8,128)S(1)}, f32[1,128,2048]{2,1,0:T(8,128)}, u32[]{:S(2)}) copy-start(f32[1,128,2048]{2,1,0:T(8,128)} %param.13) | copy-start | bytes 3145732
  265.3 6.1 %copy-start.1 = (f32[1,128,2048]{2,1,0:T(8,128)S(1)}, f32[1,128,2048]{2,1,0:T(8,128)}, u32[]{:S(2)}) copy-start(f32[1,128,2048]{2,1,0:T(8,128)} %param.15) | copy-start | bytes 3145732
  265.3 6.1 %copy-start.2 = (f32[128,2048]{1,0:T(8,128)S(1)}, f32[128,2048]{1,0:T(8,128)}, u32[]{:S(2)}) copy-start(f32[128,2048]{1,0:T(8,128)} %get-tuple-element.7) | copy-start | bytes 3145732

commit v3 on v2

--- a/solution.py
+++ b/solution.py
@@ -30,37 +30,6 @@
     return lax.broadcasted_iota(jnp.int32, shape, dim)
 
 
-def pack_kernel(dest_col, dest_row, docs, targs, out):
-    block = pl.program_id(0) % 4
-    row = dest_row[0]
-    same = jnp.where(dest_col[0] == row, 1, 0)
-    earlier = jnp.where(iota((ROWS, ROWS), 0) < iota((ROWS, ROWS), 1), same, 0)
-    rank = jnp.sum(earlier, axis=0, keepdims=True)
-    total = jnp.zeros((256, D // 2), F32)
-    for kind, source in enumerate((docs, targs)):
-        for half in range(2):
-            slot = row * 8 + (kind * 4 + half) + rank * 2 - block * 256
-            pick = jnp.where(iota((256, ROWS), 0) == slot, 1.0, 0.0).astype(BF)
-            total += jnp.dot(pick, source[0, :, half * 1024 : (half + 1) * 1024], preferred_element_type=F32)
-    out[...] = total.astype(BF)
-
-
-def pack(routes, docs, targs):
-    return pl.pallas_call(
-        pack_kernel,
-        grid=(8,),
-        out_shape=jax.ShapeDtypeStruct((2 * PATHS * 8, D // 2), BF),
-        in_specs=[
-            pl.BlockSpec((1, ROWS, 1), lambda i: (i // 4, 0, 0)),
-            pl.BlockSpec((1, 1, ROWS), lambda i: (i // 4, 0, 0)),
-            pl.BlockSpec((1, ROWS, D), lambda i: (i // 4, 0, 0)),
-            pl.BlockSpec((1, ROWS, D), lambda i: (i // 4, 0, 0)),
-        ],
-        out_specs=pl.BlockSpec((256, D // 2), lambda i: (i, 0)),
-        name="pack",
-    )(routes, routes.reshape(2, 1, ROWS), docs, targs)
-
-
 P_ROWS = 160
 Q_ROWS = 256 - P_ROWS
 
@@ -80,7 +49,8 @@
 
 
 def round_kernel(
-    counts, own_one, own_two, slots, got, avg_one, avg_two,
+    routes, counts_in, docs, targs, module_one, module_two, got, avg_one, avg_two,
+    counts,
     one, two, g_one, g_two, stage, x, y, hid, err, inn, slope, x_t, h_t,
     early_p, late_p, pair_p, y_q, early_q, late_q, core_in, early_t, late_t, pair_t,
     ring_sem, fwd_sem, y_sem, q_sem, core_sem, a2a_sem, local_sem,
@@ -121,12 +91,11 @@
     def whole(s, full, step):
         return s.at(full, step, 0, 2 * s.half)
 
-    def spread(s, full, own=None):
+    def spread(s, full):
         for way, to in ((0, s.plus), (1, s.minus)):
             for which in (0, 1) if way == 0 else (1, 0):
-                dst = s.at(full, 0, which * s.half, s.half)
-                src = dst if own is None else own.at[pl.ds(which * s.half, s.half)]
-                start(remote(src, dst, ring_sem.at[s.n, way, which], to))
+                ref = s.at(full, 0, which * s.half, s.half)
+                start(remote(ref, ref, ring_sem.at[s.n, way, which], to))
 
     def arrived(s, full, way, which):
         ref = s.at(full, 3 if way == 0 else 1, which * s.half, s.half)
@@ -147,31 +116,87 @@
             ref = s.at(full, 2, way * s.half, s.half)
             remote(ref, ref, fwd_sem.at[s.n, way], twin).wait_recv()
 
-    def q_across(step, src=None):
-        dst = whole(q0, one, step)
-        start(remote(dst if src is None else src, dst, q_sem.at[step], q0.partner))
-
-    def to_twin(s, j, step, src=None):
-        dst = whole(s, two, step)
-        start(remote(dst if src is None else src, dst, core_sem.at[step, j], twin))
-
-    own_p, own_q = own_one.at[pl.ds(0, P_ROWS)], own_one.at[pl.ds(P_ROWS, Q_ROWS)]
-    start(remote(own_p, whole(p0, one, 0), y_sem.at[0], p0.partner))
-    start(remote(own_two, whole(t0, two, 0), y_sem.at[1], t0.partner))
-    spread(p0, one, own_p)
-    spread(t0, two, own_two)
-    spread(q0, one, own_q)
-    q_across(0, own_q)
-    to_twin(t0, 0, 0, own_two)
-    locals_ = [
-        pltpu.make_async_copy(own_p, whole(p0, one, 0), local_sem.at[0]),
-        pltpu.make_async_copy(own_q, whole(q0, one, 0), local_sem.at[1]),
-        pltpu.make_async_copy(own_two, whole(t0, two, 0), local_sem.at[2]),
-        pltpu.make_async_copy(slots.at[0, me], got.at[0, me], local_sem.at[3]),
-        pltpu.make_async_copy(slots.at[1, me], got.at[1, me], local_sem.at[4]),
+    def q_across(step):
+        ref = whole(q0, one, step)
+        start(remote(ref, ref, q_sem.at[step], q0.partner))
+
+    def to_twin(s, j, step):
+        ref = whole(s, two, step)
+        start(remote(ref, ref, core_sem.at[step, j], twin))
+
+    def unpack(m):
+        o, i = iota((256, 256), 0), iota((256, 256), 1)
+        source = o % 64 // 2 * 8 + o // 128 * 4 + o % 2 * 2 + o // 64 % 2
+        pick = jnp.where(i == source, 1.0, 0.0).astype(BF)
+        loads = [
+            pltpu.make_async_copy(got.at[m, pl.ds(b * 32, 32)], stage.at[b % 2], local_sem.at[5 + b % 2]) for b in range(4)
+        ]
+        loads[0].start()
+        loads[1].start()
+        for b in range(4):
+            loads[b].wait()
+            part = stage[b % 2].reshape(256, D // 2)
+            rows = jnp.dot(pick, part, preferred_element_type=F32).astype(BF)
+            for half in range(2):
+                cols = slice(half * 1024, (half + 1) * 1024)
+                x[b * 64 : (b + 1) * 64, cols] = rows[half * 64 : half * 64 + 64]
+                y[b * 64 : (b + 1) * 64, cols] = rows[128 + half * 64 : 192 + half * 64]
+            if b < 2:
+                loads[b + 2].start()
+
+    upper = pltpu.make_async_copy(module_one.at[0, pl.ds(0, 128)], slope.at[pl.ds(0, 128)], local_sem.at[0])
+    lower = pltpu.make_async_copy(module_one.at[0, pl.ds(128, 128)], slope.at[pl.ds(0, 128)], local_sem.at[1])
+    other = pltpu.make_async_copy(module_two.at[0], slope.at[pl.ds(128, 128)], local_sem.at[2])
+    upper.start()
+    other.start()
+    loads = [
+        pltpu.make_async_copy(source.at[m], to.at[pl.ds(m * ROWS, ROWS)], local_sem.at[3 + m * 2 + n])
+        for m in range(2)
+        for n, (source, to) in enumerate(((docs, x), (targs, y)))
     ]
-    for copy in locals_:
+    loads.append(pltpu.make_async_copy(counts_in, counts, local_sem.at[7]))
+    for copy in loads:
         copy.start()
+    upper.wait()
+    p0.at(one, 0, 0, 128)[...] = slope[0:128].astype(BF)
+    lower.start()
+    other.wait()
+    whole(t0, two, 0)[...] = slope[128:256].astype(BF)
+    start(remote(whole(t0, two, 0), whole(t0, two, 0), y_sem.at[1], t0.partner))
+    lower.wait()
+    p0.at(one, 0, 128, 128)[...] = slope[0:128].astype(BF)
+    start(remote(whole(p0, one, 0), whole(p0, one, 0), y_sem.at[0], p0.partner))
+    spread(p0, one)
+    spread(t0, two)
+    spread(q0, one)
+    q_across(0)
+    to_twin(t0, 0, 0)
+    for copy in loads:
+        copy.wait()
+
+    def pack(m):
+        to = routes[m]
+        same_place = iota((ROWS, ROWS), 0) == iota((ROWS, ROWS), 1)
+        down = jnp.sum(jnp.where(same_place, to, 0), axis=1, keepdims=True)
+        same = jnp.where(down == to, 1, 0)
+        earlier = jnp.where(iota((ROWS, ROWS), 0) < iota((ROWS, ROWS), 1), same, 0)
+        rank = jnp.sum(earlier, axis=0, keepdims=True)
+
+        def block(b, carry):
+            total = jnp.zeros((256, D // 2), F32)
+            for kind, source in enumerate((x, y)):
+                for half in range(2):
+                    slot = to * 8 + (kind * 4 + half) + rank * 2 - b * 256
+                    pick = jnp.where(iota((256, ROWS), 0) == slot, 1.0, 0.0).astype(BF)
+                    part = source[m * ROWS : (m + 1) * ROWS, half * 1024 : (half + 1) * 1024]
+                    total += jnp.dot(pick, part, preferred_element_type=F32)
+            g_one[pl.ds(pl.multiple_of(b * 256, 256), 256), m * 1024 : (m + 1) * 1024] = total.astype(BF)
+            return carry
+
+        lax.fori_loop(0, 4, block, 0)
+
+    def slot_rows(m, path):
+        return g_one.at[pl.ds(pl.multiple_of(path * 8, 8), 8), pl.ds(m * 1024, 1024)]
 
     def send_slots(m):
         def send(step, carry):
@@ -183,18 +208,24 @@
                 z=(z + t // 16 % 4) % 4,
                 core=(core + t // 64) % 2,
             )
-            remote(slots.at[m, to[0] * N_COL + to[1]], got.at[m, me], a2a_sem.at[m], to).start()
+            remote(slot_rows(m, to[0] * N_COL + to[1]), got.at[m, me], a2a_sem.at[m], to).start()
             return carry
 
         lax.fori_loop(1, PATHS, send, 0)
 
     def all_slots(m):
-        return remote(slots.at[m, pl.ds(0, PATHS - 1)], got.at[m, pl.ds(0, PATHS - 1)], a2a_sem.at[m], twin)
-
-    send_slots(0)
-    remote(own_p, whole(p1, one, 0), y_sem.at[0], twin).wait_recv()
+        ref = got.at[m, pl.ds(0, PATHS - 1)]
+        return remote(ref, ref, a2a_sem.at[m], twin)
+
+    own_slots = [pltpu.make_async_copy(slot_rows(m, me), got.at[m, me], local_sem.at[m]) for m in range(2)]
+    for m in range(2):
+        pack(m)
+        own_slots[m].start()
+        if m == 0:
+            send_slots(0)
+    remote(whole(p1, one, 0), whole(p1, one, 0), y_sem.at[0], twin).wait_recv()
     spread(p1, one)
-    remote(own_two, whole(t1, two, 0), y_sem.at[1], twin).wait_recv()
+    remote(whole(t1, two, 0), whole(t1, two, 0), y_sem.at[1], twin).wait_recv()
     spread(t1, two)
     to_twin(t1, 1, 0)
     forward(p0, one)
@@ -214,7 +245,10 @@
     for j, s in ((0, t0), (1, t1)):
         forwarded(s, two)
         to_twin(s, j, 2)
-    send_slots(1)
+    for copy in own_slots:
+        copy.wait()
+    all_slots(0).wait_recv()
+    unpack(0)
     for step in range(4):
         ref = whole(q1, one, step)
         remote(ref, ref, q_sem.at[step], twin).wait_recv()
@@ -224,29 +258,7 @@
     for s in (p0, p1):
         rest(s, one)
         forwarded(s, one)
-    for copy in locals_:
-        copy.wait()
-    all_slots(0).wait_recv()
-
-    def unpack(m):
-        o, i = iota((256, 256), 0), iota((256, 256), 1)
-        source = o % 64 // 2 * 8 + o // 128 * 4 + o % 2 * 2 + o // 64 % 2
-        pick = jnp.where(i == source, 1.0, 0.0).astype(BF)
-        loads = [
-            pltpu.make_async_copy(got.at[m, pl.ds(b * 32, 32)], stage.at[b % 2], local_sem.at[5 + b % 2]) for b in range(4)
-        ]
-        loads[0].start()
-        loads[1].start()
-        for b in range(4):
-            loads[b].wait()
-            part = stage[b % 2].reshape(256, D // 2)
-            rows = jnp.dot(pick, part, preferred_element_type=F32).astype(BF)
-            for half in range(2):
-                cols = slice(half * 1024, (half + 1) * 1024)
-                x[b * 64 : (b + 1) * 64, cols] = rows[half * 64 : half * 64 + 64]
-                y[b * 64 : (b + 1) * 64, cols] = rows[128 + half * 64 : 192 + half * 64]
-            if b < 2:
-                loads[b + 2].start()
+    send_slots(1)
 
     def spans(n, tile):
         return pl.ds(pl.multiple_of(n * tile, tile), tile)
@@ -329,12 +341,13 @@
 
         lax.fori_loop(0, 4, step, 0)
 
-    unpack(0)
     passes()
     for copy in sent:
         copy.wait_send()
     sent.clear()
     first_update(h_t, err, two, g_two)
+    for m in range(2):
+        all_slots(m).wait_send()
     first_update(x_t, inn, one, g_one)
     all_slots(1).wait_recv()
     unpack(1)
@@ -393,19 +406,29 @@
     def unit_one(step):
         last_update(x_t, inn, one, g_one, share_one, (z + step) % 4 * 512)
         start(remote(whole(q1, g_one, step), y_q.at[step], yq_sem.at[step], q1.partner))
-        for s in (p1, p0):
-            if step == 2:
-                send_early(s)
-            elif step:
-                send_plain(s, step // 2)
 
     def unit_two(step):
         last_update(h_t, err, two, g_two, share_two, (xx + step) % 4 * 512)
         for j, s in ((1, u1), (0, u0)):
             start(remote(whole(s, g_two, step), core_in.at[step, j], core_two_sem.at[step, j], twin))
 
-    for step in (2, 1, 3, 0):
-        unit_one(step)
+    def to_pair(s, out, pair, n):
+        for which in range(2):
+            out[which * s.half : (which + 1) * s.half] = total(s, which).astype(BF)
+        start(remote(out, pair, pair_sem.at[n], s.partner))
+
+    out_t, out_p = y.at[pl.ds(0, 128)], x.at[pl.ds(0, P_ROWS)]
+    unit_one(2)
+    send_early(p1)
+    unit_one(1)
+    send_plain(p1, 0)
+    unit_one(3)
+    send_plain(p1, 1)
+    send_early(p0)
+    unit_one(0)
+    send_joined(p1)
+    send_plain(p0, 0)
+    send_plain(p0, 1)
     unit_two(2)
     join_q(2)
     send_early(q0)
@@ -413,8 +436,6 @@
     send_plain(q0, 0)
     join_q(3)
     send_plain(q0, 1)
-    for s in (p1, p0):
-        send_joined(s)
     for j, s in ((1, t1), (0, t0)):
         join_core(s, j, 2)
         send_early(s)
@@ -422,21 +443,19 @@
     for j, s in ((1, t1), (0, t0)):
         join_core(s, j, 1)
         send_plain(s, 0)
+    send_joined(p0)
     unit_two(3)
     for j, s in ((1, t1), (0, t0)):
         join_core(s, j, 3)
         send_plain(s, 1)
     send_joined(q0)
+    to_pair(p1, out_p, pair_p, 0)
     unit_two(0)
-    join_q(0)
     for j, s in ((1, t1), (0, t0)):
         join_core(s, j, 0)
         send_joined(s)
-    out_t, out_p = y.at[pl.ds(0, 128)], x.at[pl.ds(0, P_ROWS)]
-    for s, out, pair, n in ((t1, out_t, pair_t, 1), (p1, out_p, pair_p, 0)):
-        for which in range(2):
-            out[which * s.half : (which + 1) * s.half] = total(s, which).astype(BF)
-        start(remote(out, pair, pair_sem.at[n], s.partner))
+    join_q(0)
+    to_pair(t1, out_t, pair_t, 1)
     for which in range(2):
         first = P_ROWS + which * q0.half
         slope[first : first + q0.half] = total(q0, which)
@@ -455,12 +474,10 @@
     done.start()
     for copy in sent:
         copy.wait_send()
-    for m in range(2):
-        all_slots(m).wait_send()
     done.wait()
 
 
-def one_round(counts, own_one, own_two, slots):
+def one_round(routes, counts, docs, targs, module_one, module_two):
     sem = pltpu.SemaphoreType.DMA
     v = lambda *shape: pltpu.VMEM(shape, BF)
     act = v(SLOTS, D)
@@ -472,9 +489,10 @@
             jax.ShapeDtypeStruct((256, D), F32),
             jax.ShapeDtypeStruct((128, D), F32),
         ),
-        in_specs=[VMEM, ANY, ANY, ANY],
+        in_specs=[VMEM] + [ANY] * 5,
         out_specs=(ANY, ANY, ANY),
-        scratch_shapes=[v(D, D)] * 4
+        scratch_shapes=[pltpu.VMEM((N_ROW, N_COL), jnp.int32)]
+        + [v(D, D)] * 4
         + [v(2, 32, 8, D // 2)]
         + [act] * 5
         + [pltpu.VMEM((SLOTS, D), F32)]
@@ -482,17 +500,16 @@
         + [v(2, 2, p, D), v(2, 2, 2, p, D), v(2 * p, D)]
         + [v(4, 2 * q, D), v(2, q, D), v(2, 2, q, D)]
         + [v(4, 2, 128, D), v(2, 2, 64, D), v(2, 2, 2, 64, D), v(128, D)]
-        + [sem((5, 2, 2, 2)), sem((5, 2, 2)), sem((2, 2)), sem((4, 2)), sem((4, 2, 2)), sem((2, 2)), sem((7,))]
+        + [sem((5, 2, 2, 2)), sem((5, 2, 2)), sem((2, 2)), sem((4, 2)), sem((4, 2, 2)), sem((2, 2)), sem((8,))]
         + [sem((5, 2, 2)), sem((5, 2, 2, 2)), sem((2, 2)), sem((4, 2)), sem((4, 2, 2))],
         compiler_params=pltpu.CompilerParams(has_side_effects=True, vmem_limit_bytes=67043328),
         name="round",
-    )(counts, own_one, own_two, slots)
+    )(routes, counts, docs, targs, module_one, module_two)
 
 
 def shards(documents, targets, routes, doc_counts, module_one, module_two, moment_one, moment_two):
-    slots = pack(routes, documents, targets)
     got, avg_one, avg_two = one_round(
-        doc_counts, module_one[0].astype(BF), module_two[0].astype(BF), slots.reshape(2, PATHS, 8, D // 2)
+        routes.reshape(2, 1, ROWS), doc_counts, documents, targets, module_one, module_two
     )
     next_moment_one = outer_moment * moment_one + avg_one[None]
     next_moment_two = outer_moment * moment_two + avg_two[None]

time: 273 us -> 239 us (0.88); the launches traced: 273 us -> 234 us
  Pallas kernels: 257 us -> 224 us
  other arithmetic: 12.6 us -> 7.76 us
    pallas_call x1, Pallas kernels: 248 us -> 224 us  [one_round(): pl.pallas_call(round_kernel, out_shape=(jax.ShapeDtypeStruct((2, PATHS, 8...]
    pallas_call x1 -> x0, Pallas kernels: 9.15 us -> none  [pack(): pl.pallas_call(pack_kernel, grid=(8,), out_shape=jax.ShapeDtypeStruct((2...]
    convert_element_type x2 -> x0, other arithmetic: 4.8 us -> none  [the longest x1 2.71 us: shards(): module_one[0].astype(BF)]
where the time goes in v3:
time: 239 us; the launch traced here: 234 us
  Pallas kernels  224 us (94%)
  other arithmetic  7.76 us (3%)
    pallas_call x1, Pallas kernels, one_round(): pl.pallas_call(round_kernel, out_shape=(jax.ShapeDtypeStruct((2, PATHS, 8...  224 us
    sub x1, other arithmetic, shards(): module_one - outer_rate * (outer_moment * next_moment_one + avg_one[None])  6.09 us

profile of v3, /device:TPU:0, one launch (start us, length us, event | category | flops | bytes accessed | tf_op | source)
XLA Modules:
  0.0 233.8 jit_solution(1825709605283063130)
XLA Ops:
  0.6 1.4 copy.12.counts_in
  2.0 224.0 %round.1 = (bf16[2,128,8,1024]{3,2,1,0:T(8,128)(2,1)}, f32[256,2048]{1,0:T(8,128)}, f32[128,2048]{1,0:T(8,128)}) custom-call(s32[2,1,128]{2,1,0:T(1,128)} %bitcast.17, s32[16,8]{1,0:T(8,128)} %copy.12.counts_in, bf16[2,128,2048]{2,1,0:T(8,128)(2,1)} %docs.1, bf16[2,128,2048]{2,1,0:T(8,128)(2,1)} %targs.1, f32[1,256,2048]{2,1,0:T(8,128)} %module_one.1, ...), custom_call_target="tpu_custom_call" | custom-call | tf_op jit(solution)/shard_map/round/pallas_call | solution.py:485
  226.0 0.0 copy-start
  226.0 0.0 copy-start.1
  226.0 0.0 copy-start.2
  226.1 6.1 %fusion.1 = (f32[1,256,2048]{2,1,0:T(8,128)}, f32[1,256,2048]{2,1,0:T(8,128)}) fusion(f32[1,256,2048]{2,1,0:T(8,128)} %module_one.1, f32[256,2048]{1,0:T(8,128)} %get-tuple-element.6, f32[1,256,2048]{2,1,0:T(8,128)} %param.14), kind=kLoop, calls=%fused_computation.3 | loop fusion | flops 3145728 | bytes 10485760 | tf_op jit(solution)/shard_map/sub | solution.py:516
  232.2 0.0 copy-done
  232.2 0.0 copy-done.1
  232.2 0.0 copy-done.2
  232.2 1.7 fusion.3
Async XLA Ops:
  226.0 6.1 %copy-start = (f32[1,128,2048]{2,1,0:T(8,128)S(1)}, f32[1,128,2048]{2,1,0:T(8,128)}, u32[]{:S(2)}) copy-start(f32[1,128,2048]{2,1,0:T(8,128)} %module_two.1) | copy-start | bytes 3145732
  226.0 6.1 %copy-start.1 = (f32[1,128,2048]{2,1,0:T(8,128)S(1)}, f32[1,128,2048]{2,1,0:T(8,128)}, u32[]{:S(2)}) copy-start(f32[1,128,2048]{2,1,0:T(8,128)} %param.15) | copy-start | bytes 3145732
  226.0 6.1 %copy-start.2 = (f32[128,2048]{1,0:T(8,128)S(1)}, f32[128,2048]{1,0:T(8,128)}, u32[]{:S(2)}) copy-start(f32[128,2048]{1,0:T(8,128)} %get-tuple-element.7) | copy-start | bytes 3145732

commit v4 on v3

--- a/solution.py
+++ b/solution.py
@@ -30,6 +30,7 @@
     return lax.broadcasted_iota(jnp.int32, shape, dim)
 
 
+P_GATHER = 160
 P_ROWS = 160
 Q_ROWS = 256 - P_ROWS
 
@@ -39,7 +40,7 @@
         self.__dict__.update(fields)
 
     def at(self, full, step, first, count):
-        return full.at[pl.ds(pl.multiple_of(self.rows((self.place + step) % 4), 16) + first, count)]
+        return full.at[pl.ds(pl.multiple_of(self.rows((self.place + step) % 4) + first, 8), count)]
 
 
 def remote(src, dst, sems, device):
@@ -74,10 +75,12 @@
     def rows_two(j, core=core):
         return lambda place: (place * 4 + ((low + j) % 2) * 2 + core) * 128
 
-    p0 = Stream(n=0, half=P_ROWS // 2, rows=rows_one(0, 0), **ring_one)
-    p1 = Stream(n=1, half=P_ROWS // 2, rows=rows_one(0, 1), **ring_one)
-    q0 = Stream(n=2, half=Q_ROWS // 2, rows=rows_one(P_ROWS, 0), **ring_one)
-    q1 = Stream(half=Q_ROWS // 2, rows=rows_one(P_ROWS, 1), **ring_one)
+    def parts_one(rows):
+        p = [Stream(n=j, half=rows // 2, rows=rows_one(0, j), **ring_one) for j in range(2)]
+        q = [Stream(n=2, half=128 - rows // 2, rows=rows_one(rows, j), **ring_one) for j in range(2)]
+        return p + q
+
+    p0, p1, q0, q1 = parts_one(P_GATHER)
     t0 = Stream(n=3, half=64, rows=rows_two(0), **ring_two)
     t1 = Stream(n=4, half=64, rows=rows_two(1), **ring_two)
     u0 = Stream(half=64, rows=rows_two(0, 1 - core), **ring_two)
@@ -313,9 +316,9 @@
         lax.fori_loop(0, 8, step, 0)
 
     tally = counts[...].astype(F32)
-    in_row = jnp.where(iota((N_ROW, N_COL), 0) == row, tally, 0.0)
-    in_col = jnp.where(iota((N_ROW, N_COL), 1) == col, tally, 0.0)
-    mine = jnp.where(iota((N_ROW, N_COL), 1) == col, in_row, 0.0)
+    in_row = jnp.where(iota((N_COL, N_ROW), 1) == row, tally, 0.0)
+    in_col = jnp.where(iota((N_COL, N_ROW), 0) == col, tally, 0.0)
+    mine = jnp.where(iota((N_COL, N_ROW), 0) == col, in_row, 0.0)
 
     def grand(v):
         return jnp.sum(jnp.sum(v, axis=0, keepdims=True), axis=1, keepdims=True)
@@ -353,6 +356,7 @@
     unpack(1)
     passes()
 
+    p0, p1, q0, q1 = parts_one(P_ROWS)
     for s, full, early, late in (
         (p0, g_one, early_p.at[0], late_p.at[0]),
         (p1, g_one, early_p.at[1], late_p.at[1]),
@@ -418,6 +422,10 @@
         start(remote(out, pair, pair_sem.at[n], s.partner))
 
     out_t, out_p = y.at[pl.ds(0, 128)], x.at[pl.ds(0, P_ROWS)]
+    def joins(step):
+        for j, s in ((1, t1), (0, t0)):
+            join_core(s, j, step)
+
     unit_one(2)
     send_early(p1)
     unit_one(1)
@@ -425,36 +433,36 @@
     unit_one(3)
     send_plain(p1, 1)
     send_early(p0)
-    unit_one(0)
+    unit_two(2)
     send_joined(p1)
     send_plain(p0, 0)
     send_plain(p0, 1)
-    unit_two(2)
+    unit_two(1)
+    joins(2)
+    send_early(t1)
+    send_early(t0)
     join_q(2)
     send_early(q0)
+    unit_one(0)
+    joins(1)
+    send_plain(t1, 0)
+    send_plain(t0, 0)
     join_q(1)
     send_plain(q0, 0)
+    unit_two(3)
+    send_joined(p0)
     join_q(3)
     send_plain(q0, 1)
-    for j, s in ((1, t1), (0, t0)):
-        join_core(s, j, 2)
-        send_early(s)
-    unit_two(1)
-    for j, s in ((1, t1), (0, t0)):
-        join_core(s, j, 1)
-        send_plain(s, 0)
-    send_joined(p0)
-    unit_two(3)
-    for j, s in ((1, t1), (0, t0)):
-        join_core(s, j, 3)
-        send_plain(s, 1)
+    unit_two(0)
+    joins(3)
+    send_plain(t1, 1)
+    send_joined(t1)
+    send_plain(t0, 1)
+    send_joined(t0)
+    to_pair(p1, out_p, pair_p, 0)
+    joins(0)
+    join_q(0)
     send_joined(q0)
-    to_pair(p1, out_p, pair_p, 0)
-    unit_two(0)
-    for j, s in ((1, t1), (0, t0)):
-        join_core(s, j, 0)
-        send_joined(s)
-    join_q(0)
     to_pair(t1, out_t, pair_t, 1)
     for which in range(2):
         first = P_ROWS + which * q0.half
@@ -491,7 +499,7 @@
         ),
         in_specs=[VMEM] + [ANY] * 5,
         out_specs=(ANY, ANY, ANY),
-        scratch_shapes=[pltpu.VMEM((N_ROW, N_COL), jnp.int32)]
+        scratch_shapes=[pltpu.VMEM((N_COL, N_ROW), jnp.int32)]
         + [v(D, D)] * 4
         + [v(2, 32, 8, D // 2)]
         + [act] * 5
@@ -509,7 +517,7 @@
 
 def shards(documents, targets, routes, doc_counts, module_one, module_two, moment_one, moment_two):
     got, avg_one, avg_two = one_round(
-        routes.reshape(2, 1, ROWS), doc_counts, documents, targets, module_one, module_two
+        routes.reshape(2, 1, ROWS), doc_counts.T, documents, targets, module_one, module_two
     )
     next_moment_one = outer_moment * moment_one + avg_one[None]
     next_moment_two = outer_moment * moment_two + avg_two[None]

time: 239 us -> 229 us (0.958)
  the two profiles are of different devices: /device:TPU:0 before, /device:TPU:110 now
where the time goes in v4:
time: 229 us
  Pallas kernels  220 us (96%)
  other arithmetic  7.76 us (3%)
    pallas_call x1, Pallas kernels, one_round(): pl.pallas_call(round_kernel, out_shape=(jax.ShapeDtypeStruct((2, PATHS, 8...  220 us
    sub x1, other arithmetic, shards(): module_one - outer_rate * (outer_moment * next_moment_one + avg_one[None])  6.09 us

profile of v4, /device:TPU:110, one launch (start us, length us, event | category | flops | bytes accessed | tf_op | source)
XLA Modules:
  0.0 228.5 jit_solution(5458026738666575292)
XLA Ops:
  0.6 220.1 %round.1 = (bf16[2,128,8,1024]{3,2,1,0:T(8,128)(2,1)}, f32[256,2048]{1,0:T(8,128)}, f32[128,2048]{1,0:T(8,128)}) custom-call(s32[2,1,128]{2,1,0:T(1,128)} %bitcast.19, s32[8,16]{1,0:T(8,128)} %bitcast.18, bf16[2,128,2048]{2,1,0:T(8,128)(2,1)} %docs.1, bf16[2,128,2048]{2,1,0:T(8,128)(2,1)} %targs.1, f32[1,256,2048]{2,1,0:T(8,128)} %module_one.1, ...), custom_call_target="tpu_custom_call" | custom-call | tf_op jit(solution)/shard_map/round/pallas_call | solution.py:493
  220.7 0.0 copy-start
  220.7 0.0 copy-start.1
  220.7 0.0 copy-start.2
  220.7 6.1 %fusion.1 = (f32[1,256,2048]{2,1,0:T(8,128)}, f32[1,256,2048]{2,1,0:T(8,128)}) fusion(f32[1,256,2048]{2,1,0:T(8,128)} %module_one.1, f32[256,2048]{1,0:T(8,128)} %get-tuple-element.6, f32[1,256,2048]{2,1,0:T(8,128)} %param.14), kind=kLoop, calls=%fused_computation.3 | loop fusion | flops 3145728 | bytes 10485760 | tf_op jit(solution)/shard_map/sub | solution.py:524
  226.8 0.0 copy-done
  226.8 0.0 copy-done.1
  226.8 0.0 copy-done.2
  226.8 1.7 fusion.3
Async XLA Ops:
  220.7 6.1 %copy-start = (f32[1,128,2048]{2,1,0:T(8,128)S(1)}, f32[1,128,2048]{2,1,0:T(8,128)}, u32[]{:S(2)}) copy-start(f32[1,128,2048]{2,1,0:T(8,128)} %module_two.1) | copy-start | bytes 3145732
  220.7 6.1 %copy-start.1 = (f32[1,128,2048]{2,1,0:T(8,128)S(1)}, f32[1,128,2048]{2,1,0:T(8,128)}, u32[]{:S(2)}) copy-start(f32[1,128,2048]{2,1,0:T(8,128)} %param.15) | copy-start | bytes 3145732
  220.7 6.1 %copy-start.2 = (f32[128,2048]{1,0:T(8,128)S(1)}, f32[128,2048]{1,0:T(8,128)}, u32[]{:S(2)}) copy-start(f32[128,2048]{1,0:T(8,128)} %get-tuple-element.7) | copy-start | bytes 3145732

commit v5 on v4

--- a/solution.py
+++ b/solution.py
@@ -147,6 +147,21 @@
             if b < 2:
                 loads[b + 2].start()
 
+    barrier = pltpu.get_barrier_semaphore()
+
+    def torus(t):
+        return device(
+            x=(xx + t % 4) % 4,
+            low=(low + t // 4 % 2) % 2,
+            high=(high + t // 8 % 2) % 2,
+            z=(z + t // 16 % 4) % 4,
+            core=(core + t // 64) % 2,
+        )
+
+    def greet(step, carry):
+        pl.semaphore_signal(barrier, inc=1, device_id=torus(step), device_id_type=MESH)
+        return carry
+
     upper = pltpu.make_async_copy(module_one.at[0, pl.ds(0, 128)], slope.at[pl.ds(0, 128)], local_sem.at[0])
     lower = pltpu.make_async_copy(module_one.at[0, pl.ds(128, 128)], slope.at[pl.ds(0, 128)], local_sem.at[1])
     other = pltpu.make_async_copy(module_two.at[0], slope.at[pl.ds(128, 128)], local_sem.at[2])
@@ -160,15 +175,17 @@
     loads.append(pltpu.make_async_copy(counts_in, counts, local_sem.at[7]))
     for copy in loads:
         copy.start()
+    lax.fori_loop(1, PATHS, greet, 0)
     upper.wait()
     p0.at(one, 0, 0, 128)[...] = slope[0:128].astype(BF)
     lower.start()
     other.wait()
     whole(t0, two, 0)[...] = slope[128:256].astype(BF)
-    start(remote(whole(t0, two, 0), whole(t0, two, 0), y_sem.at[1], t0.partner))
     lower.wait()
     p0.at(one, 0, 128, 128)[...] = slope[0:128].astype(BF)
+    pl.semaphore_wait(barrier, PATHS - 1)
     start(remote(whole(p0, one, 0), whole(p0, one, 0), y_sem.at[0], p0.partner))
+    start(remote(whole(t0, two, 0), whole(t0, two, 0), y_sem.at[1], t0.partner))
     spread(p0, one)
     spread(t0, two)
     spread(q0, one)
@@ -204,13 +221,7 @@
     def send_slots(m):
         def send(step, carry):
             t = step * 53 % PATHS
-            to = device(
-                x=(xx + t % 4) % 4,
-                low=(low + t // 4 % 2) % 2,
-                high=(high + t // 8 % 2) % 2,
-                z=(z + t // 16 % 4) % 4,
-                core=(core + t // 64) % 2,
-            )
+            to = torus(t)
             remote(slot_rows(m, to[0] * N_COL + to[1]), got.at[m, me], a2a_sem.at[m], to).start()
             return carry
 
@@ -510,7 +521,7 @@
         + [v(4, 2, 128, D), v(2, 2, 64, D), v(2, 2, 2, 64, D), v(128, D)]
         + [sem((5, 2, 2, 2)), sem((5, 2, 2)), sem((2, 2)), sem((4, 2)), sem((4, 2, 2)), sem((2, 2)), sem((8,))]
         + [sem((5, 2, 2)), sem((5, 2, 2, 2)), sem((2, 2)), sem((4, 2)), sem((4, 2, 2))],
-        compiler_params=pltpu.CompilerParams(has_side_effects=True, vmem_limit_bytes=67043328),
+        compiler_params=pltpu.CompilerParams(has_side_effects=True, collective_id=0, vmem_limit_bytes=67043328),
         name="round",
     )(routes, counts, docs, targs, module_one, module_two)
 

time: 229 us -> 221 us (0.965)
  the two profiles are of different devices: /device:TPU:110 before, /device:TPU:0 now
where the time goes in v5:
time: 221 us; the launch traced here: 220 us
  Pallas kernels  212 us (96%)
  other arithmetic  7.76 us (4%)
    pallas_call x1, Pallas kernels, one_round(): pl.pallas_call(round_kernel, out_shape=(jax.ShapeDtypeStruct((2, PATHS, 8...  212 us
    sub x1, other arithmetic, shards(): module_one - outer_rate * (outer_moment * next_moment_one + avg_one[None])  6.09 us

profile of v5, /device:TPU:0, one launch (start us, length us, event | category | flops | bytes accessed | tf_op | source)
XLA Modules:
  0.0 220.4 jit_solution(18420706038226790263)
XLA Ops:
  0.6 212.0 %round.1 = (bf16[2,128,8,1024]{3,2,1,0:T(8,128)(2,1)}, f32[256,2048]{1,0:T(8,128)}, f32[128,2048]{1,0:T(8,128)}) custom-call(s32[2,1,128]{2,1,0:T(1,128)} %bitcast.19, s32[8,16]{1,0:T(8,128)} %bitcast.18, bf16[2,128,2048]{2,1,0:T(8,128)(2,1)} %docs.1, bf16[2,128,2048]{2,1,0:T(8,128)(2,1)} %targs.1, f32[1,256,2048]{2,1,0:T(8,128)} %module_one.1, ...), custom_call_target="tpu_custom_call" | custom-call | tf_op jit(solution)/shard_map/round/pallas_call | solution.py:504
  212.6 0.0 copy-start
  212.6 0.0 copy-start.1
  212.6 0.0 copy-start.2
  212.7 6.1 %fusion.1 = (f32[1,256,2048]{2,1,0:T(8,128)}, f32[1,256,2048]{2,1,0:T(8,128)}) fusion(f32[1,256,2048]{2,1,0:T(8,128)} %module_one.1, f32[256,2048]{1,0:T(8,128)} %get-tuple-element.6, f32[1,256,2048]{2,1,0:T(8,128)} %param.14), kind=kLoop, calls=%fused_computation.3 | loop fusion | flops 3145728 | bytes 10485760 | tf_op jit(solution)/shard_map/sub | solution.py:535
  218.7 0.0 copy-done
  218.7 0.0 copy-done.1
  218.7 0.0 copy-done.2
  218.8 1.7 fusion.3
Async XLA Ops:
  212.6 6.1 %copy-start = (f32[1,128,2048]{2,1,0:T(8,128)S(1)}, f32[1,128,2048]{2,1,0:T(8,128)}, u32[]{:S(2)}) copy-start(f32[1,128,2048]{2,1,0:T(8,128)} %module_two.1) | copy-start | bytes 3145732
  212.6 6.1 %copy-start.1 = (f32[1,128,2048]{2,1,0:T(8,128)S(1)}, f32[1,128,2048]{2,1,0:T(8,128)}, u32[]{:S(2)}) copy-start(f32[1,128,2048]{2,1,0:T(8,128)} %param.15) | copy-start | bytes 3145732
  212.6 6.1 %copy-start.2 = (f32[128,2048]{1,0:T(8,128)S(1)}, f32[128,2048]{1,0:T(8,128)}, u32[]{:S(2)}) copy-start(f32[128,2048]{1,0:T(8,128)} %get-tuple-element.7) | copy-start | bytes 3145732

commit v6 on v5

--- a/solution.py
+++ b/solution.py
@@ -50,12 +50,12 @@
 
 
 def round_kernel(
-    routes, counts_in, docs, targs, module_one, module_two, got, avg_one, avg_two,
+    routes, counts_in, docs, targs, module_one, module_two, got, packed, avg_one, avg_two,
     counts,
     one, two, g_one, g_two, stage, x, y, hid, err, inn, slope, x_t, h_t,
     early_p, late_p, pair_p, y_q, early_q, late_q, core_in, early_t, late_t, pair_t,
     ring_sem, fwd_sem, y_sem, q_sem, core_sem, a2a_sem, local_sem,
-    early_sem, late_sem, pair_sem, yq_sem, core_two_sem,
+    early_sem, late_sem, pair_sem, yq_sem, core_two_sem, pack_sem, own_sem,
 ):
     row, col = lax.axis_index("row"), lax.axis_index("col")
     xx, low, core = row // 4, (row // 2) % 2, row % 2
@@ -127,39 +127,34 @@
         ref = whole(s, two, step)
         start(remote(ref, ref, core_sem.at[step, j], twin))
 
-    def unpack(m):
+    def unpack(ch, into):
         o, i = iota((256, 256), 0), iota((256, 256), 1)
-        source = o % 64 // 2 * 8 + o // 128 * 4 + o % 2 * 2 + o // 64 % 2
+        source = o % 64 // 2 * 8 + o % 2 * 4 + o // 64
         pick = jnp.where(i == source, 1.0, 0.0).astype(BF)
         loads = [
-            pltpu.make_async_copy(got.at[m, pl.ds(b * 32, 32)], stage.at[b % 2], local_sem.at[5 + b % 2]) for b in range(4)
+            pltpu.make_async_copy(got.at[ch, pl.ds(b * 32, 32)], stage.at[b], local_sem.at[b]) for b in range(4)
         ]
-        loads[0].start()
-        loads[1].start()
+        for copy in loads:
+            copy.start()
         for b in range(4):
             loads[b].wait()
-            part = stage[b % 2].reshape(256, D // 2)
-            rows = jnp.dot(pick, part, preferred_element_type=F32).astype(BF)
-            for half in range(2):
-                cols = slice(half * 1024, (half + 1) * 1024)
-                x[b * 64 : (b + 1) * 64, cols] = rows[half * 64 : half * 64 + 64]
-                y[b * 64 : (b + 1) * 64, cols] = rows[128 + half * 64 : 192 + half * 64]
-            if b < 2:
-                loads[b + 2].start()
+            rows = jnp.dot(pick, stage[b].reshape(256, 512), preferred_element_type=F32).astype(BF)
+            for quarter in range(4):
+                cols = slice(quarter * 512, (quarter + 1) * 512)
+                into[b * 64 : (b + 1) * 64, cols] = rows[quarter * 64 : (quarter + 1) * 64]
 
     barrier = pltpu.get_barrier_semaphore()
 
-    def torus(t):
-        return device(
-            x=(xx + t % 4) % 4,
-            low=(low + t // 4 % 2) % 2,
-            high=(high + t // 8 % 2) % 2,
-            z=(z + t // 16 % 4) % 4,
-            core=(core + t // 64) % 2,
-        )
-
     def greet(step, carry):
-        pl.semaphore_signal(barrier, inc=1, device_id=torus(step), device_id_type=MESH)
+        for n in range(8):
+            to = device(
+                x=(xx + n % 4) % 4,
+                low=(low + n // 4) % 2,
+                high=(high + step % 2) % 2,
+                z=(z + step // 2 % 4) % 4,
+                core=(core + step // 8) % 2,
+            )
+            pl.semaphore_signal(barrier, inc=1, device_id=to, device_id_type=MESH)
         return carry
 
     upper = pltpu.make_async_copy(module_one.at[0, pl.ds(0, 128)], slope.at[pl.ds(0, 128)], local_sem.at[0])
@@ -175,7 +170,10 @@
     loads.append(pltpu.make_async_copy(counts_in, counts, local_sem.at[7]))
     for copy in loads:
         copy.start()
-    lax.fori_loop(1, PATHS, greet, 0)
+    for n in range(1, 8):
+        to = device(x=(xx + n % 4) % 4, low=(low + n // 4) % 2)
+        pl.semaphore_signal(barrier, inc=1, device_id=to, device_id_type=MESH)
+    lax.fori_loop(1, 16, greet, 0)
     upper.wait()
     p0.at(one, 0, 0, 128)[...] = slope[0:128].astype(BF)
     lower.start()
@@ -203,40 +201,61 @@
         rank = jnp.sum(earlier, axis=0, keepdims=True)
 
         def block(b, carry):
-            total = jnp.zeros((256, D // 2), F32)
             for kind, source in enumerate((x, y)):
-                for half in range(2):
-                    slot = to * 8 + (kind * 4 + half) + rank * 2 - b * 256
+                total = jnp.zeros((256, 512), F32)
+                for quarter in range(4):
+                    slot = to * 8 + rank * 4 + quarter - b * 256
                     pick = jnp.where(iota((256, ROWS), 0) == slot, 1.0, 0.0).astype(BF)
-                    part = source[m * ROWS : (m + 1) * ROWS, half * 1024 : (half + 1) * 1024]
+                    part = source[m * ROWS : (m + 1) * ROWS, quarter * 512 : (quarter + 1) * 512]
                     total += jnp.dot(pick, part, preferred_element_type=F32)
-            g_one[pl.ds(pl.multiple_of(b * 256, 256), 256), m * 1024 : (m + 1) * 1024] = total.astype(BF)
+                rows = pl.ds(pl.multiple_of(b * 256, 256), 256)
+                g_one[rows, (m * 2 + kind) * 512 : (m * 2 + kind + 1) * 512] = total.astype(BF)
             return carry
 
         lax.fori_loop(0, 4, block, 0)
+        for kind in range(2):
+            pltpu.make_async_copy(packed_part(m * 2 + kind), packed.at[m * 2 + kind], pack_sem.at[m * 2 + kind]).start()
+        for kind in range(2):
+            pltpu.make_async_copy(packed_part(m * 2 + kind), packed.at[m * 2 + kind], pack_sem.at[m * 2 + kind]).wait()
+
+    def packed_part(ch):
+        return g_one.at[pl.ds(0, PATHS * 8), pl.ds(ch * 512, 512)]
 
     def slot_rows(m, path):
-        return g_one.at[pl.ds(pl.multiple_of(path * 8, 8), 8), pl.ds(m * 1024, 1024)]
+        return packed.at[m, pl.ds(pl.multiple_of(path * 8, 8), 8)]
+
+    row_of = [(xx + n % 4) % 4 * 4 + (low + n // 4) % 2 * 2 for n in range(8)]
 
     def send_slots(m):
-        def send(step, carry):
-            t = step * 53 % PATHS
-            to = torus(t)
+        def send(turn, n):
+            t = n * 53 % PATHS
+            u = lax.rem(turn * 5 + t // 8, 16)
+            to_high = lax.rem(high + lax.rem(u, 2), 2)
+            to_z = lax.rem(z + lax.rem(lax.div(u, 2), 4), 4)
+            to_core = lax.rem(core + lax.div(u, 8), 2)
+            to = (row_of[t % 8] + to_core, to_z * 2 + to_high)
             remote(slot_rows(m, to[0] * N_COL + to[1]), got.at[m, me], a2a_sem.at[m], to).start()
-            return carry
-
-        lax.fori_loop(1, PATHS, send, 0)
+
+        def eight(turn, carry):
+            for n in range(8):
+                send(turn, n)
+            return carry
+
+        for n in range(1, 8):
+            send(jnp.int32(0), n)
+        lax.fori_loop(1, 16, eight, 0)
 
     def all_slots(m):
         ref = got.at[m, pl.ds(0, PATHS - 1)]
         return remote(ref, ref, a2a_sem.at[m], twin)
 
-    own_slots = [pltpu.make_async_copy(slot_rows(m, me), got.at[m, me], local_sem.at[m]) for m in range(2)]
+    own_slots = [pltpu.make_async_copy(slot_rows(ch, me), got.at[ch, me], own_sem.at[ch]) for ch in range(4)]
     for m in range(2):
         pack(m)
-        own_slots[m].start()
-        if m == 0:
-            send_slots(0)
+        for kind in range(2):
+            own_slots[m * 2 + kind].start()
+            if m == 0:
+                send_slots(kind)
     remote(whole(p1, one, 0), whole(p1, one, 0), y_sem.at[0], twin).wait_recv()
     spread(p1, one)
     remote(whole(t1, two, 0), whole(t1, two, 0), y_sem.at[1], twin).wait_recv()
@@ -262,7 +281,9 @@
     for copy in own_slots:
         copy.wait()
     all_slots(0).wait_recv()
-    unpack(0)
+    unpack(0, x)
+    all_slots(1).wait_recv()
+    unpack(1, y)
     for step in range(4):
         ref = whole(q1, one, step)
         remote(ref, ref, q_sem.at[step], twin).wait_recv()
@@ -272,14 +293,14 @@
     for s in (p0, p1):
         rest(s, one)
         forwarded(s, one)
-    send_slots(1)
+    send_slots(2)
 
     def spans(n, tile):
         return pl.ds(pl.multiple_of(n * tile, tile), tile)
 
-    def passes():
-        wide = 1024
-
+    wide = 1024
+
+    def pre_pass():
         def pre_tile(n, carry):
             cols = spans(n, wide)
             pre = jnp.dot(x[...], one[:, cols], preferred_element_type=F32) * SCALE
@@ -290,6 +311,7 @@
 
         lax.fori_loop(0, D // wide, pre_tile, 0)
 
+    def err_pass():
         def err_tile(n, carry):
             cols = spans(n, wide)
             out = jnp.dot(hid[...], two[:, cols], preferred_element_type=F32) * SCALE
@@ -307,6 +329,7 @@
 
         lax.fori_loop(0, D // wide, inn_tile, 0)
 
+    def turns():
         def turn(n, carry):
             cols = spans(n, 256)
             x_t[cols, :] = x[:, cols].T
@@ -355,17 +378,24 @@
 
         lax.fori_loop(0, 4, step, 0)
 
-    passes()
+    pre_pass()
+    err_pass()
+    turns()
+    send_slots(3)
     for copy in sent:
         copy.wait_send()
     sent.clear()
+    first_update(x_t, inn, one, g_one)
+    all_slots(2).wait_recv()
+    unpack(2, x)
+    pre_pass()
     first_update(h_t, err, two, g_two)
-    for m in range(2):
-        all_slots(m).wait_send()
-    first_update(x_t, inn, one, g_one)
-    all_slots(1).wait_recv()
-    unpack(1)
-    passes()
+    turns()
+    all_slots(3).wait_recv()
+    unpack(3, y)
+    err_pass()
+    for ch in range(4):
+        all_slots(ch).wait_send()
 
     p0, p1, q0, q1 = parts_one(P_ROWS)
     for s, full, early, late in (
@@ -504,30 +534,31 @@
     return pl.pallas_call(
         round_kernel,
         out_shape=(
-            jax.ShapeDtypeStruct((2, PATHS, 8, D // 2), BF),
+            jax.ShapeDtypeStruct((4, PATHS, 8, D // 4), BF),
+            jax.ShapeDtypeStruct((4, PATHS * 8, D // 4), BF),
             jax.ShapeDtypeStruct((256, D), F32),
             jax.ShapeDtypeStruct((128, D), F32),
         ),
         in_specs=[VMEM] + [ANY] * 5,
-        out_specs=(ANY, ANY, ANY),
+        out_specs=(ANY, ANY, ANY, ANY),
         scratch_shapes=[pltpu.VMEM((N_COL, N_ROW), jnp.int32)]
         + [v(D, D)] * 4
-        + [v(2, 32, 8, D // 2)]
+        + [v(4, 32, 8, D // 4)]
         + [act] * 5
         + [pltpu.VMEM((SLOTS, D), F32)]
         + [v(D, SLOTS)] * 2
         + [v(2, 2, p, D), v(2, 2, 2, p, D), v(2 * p, D)]
         + [v(4, 2 * q, D), v(2, q, D), v(2, 2, q, D)]
         + [v(4, 2, 128, D), v(2, 2, 64, D), v(2, 2, 2, 64, D), v(128, D)]
-        + [sem((5, 2, 2, 2)), sem((5, 2, 2)), sem((2, 2)), sem((4, 2)), sem((4, 2, 2)), sem((2, 2)), sem((8,))]
-        + [sem((5, 2, 2)), sem((5, 2, 2, 2)), sem((2, 2)), sem((4, 2)), sem((4, 2, 2))],
+        + [sem((5, 2, 2, 2)), sem((5, 2, 2)), sem((2, 2)), sem((4, 2)), sem((4, 2, 2)), sem((4, 2)), sem((8,))]
+        + [sem((5, 2, 2)), sem((5, 2, 2, 2)), sem((2, 2)), sem((4, 2)), sem((4, 2, 2)), sem((4,)), sem((4,))],
         compiler_params=pltpu.CompilerParams(has_side_effects=True, collective_id=0, vmem_limit_bytes=67043328),
         name="round",
     )(routes, counts, docs, targs, module_one, module_two)
 
 
 def shards(documents, targets, routes, doc_counts, module_one, module_two, moment_one, moment_two):
-    got, avg_one, avg_two = one_round(
+    got, packed, avg_one, avg_two = one_round(
         routes.reshape(2, 1, ROWS), doc_counts.T, documents, targets, module_one, module_two
     )
     next_moment_one = outer_moment * moment_one + avg_one[None]

time: 221 us -> 216 us (0.977)
  Pallas kernels: 212 us -> 207 us
    pallas_call x1, Pallas kernels: 212 us -> 207 us  [one_round(): pl.pallas_call(round_kernel, out_shape=(jax.ShapeDtypeStruct((4, PATHS, 8...]
where the time goes in v6:
time: 216 us
  Pallas kernels  207 us (96%)
  other arithmetic  7.76 us (4%)
    pallas_call x1, Pallas kernels, one_round(): pl.pallas_call(round_kernel, out_shape=(jax.ShapeDtypeStruct((4, PATHS, 8...  207 us
    sub x1, other arithmetic, shards(): module_one - outer_rate * (outer_moment * next_moment_one + avg_one[None])  6.09 us

profile of v6, /device:TPU:0, one launch (start us, length us, event | category | flops | bytes accessed | tf_op | source)
XLA Modules:
  0.0 215.6 jit_solution(12038359457020038081)
XLA Ops:
  0.6 207.2 %round.1 = (bf16[4,128,8,512]{3,2,1,0:T(8,128)(2,1)}, bf16[4,1024,512]{2,1,0:T(8,128)(2,1)}, f32[256,2048]{1,0:T(8,128)}, f32[128,2048]{1,0:T(8,128)}) custom-call(s32[2,1,128]{2,1,0:T(1,128)} %bitcast.19, s32[8,16]{1,0:T(8,128)} %bitcast.18, bf16[2,128,2048]{2,1,0:T(8,128)(2,1)} %docs.1, bf16[2,128,2048]{2,1,0:T(8,128)(2,1)} %targs.1, ...), custom_call_target="tpu_custom_call" | custom-call | tf_op jit(solution)/shard_map/round/pallas_call | solution.py:534
  207.8 0.0 copy-start
  207.8 0.0 copy-start.1
  207.8 0.0 copy-start.2
  207.9 6.1 %fusion.1 = (f32[1,256,2048]{2,1,0:T(8,128)}, f32[1,256,2048]{2,1,0:T(8,128)}) fusion(f32[1,256,2048]{2,1,0:T(8,128)} %module_one.1, f32[256,2048]{1,0:T(8,128)} %get-tuple-element.6, f32[1,256,2048]{2,1,0:T(8,128)} %param.14), kind=kLoop, calls=%fused_computation.3 | loop fusion | flops 3145728 | bytes 10485760 | tf_op jit(solution)/shard_map/sub | solution.py:566
  213.9 0.0 copy-done
  213.9 0.0 copy-done.1
  214.0 0.0 copy-done.2
  214.0 1.7 fusion.3
Async XLA Ops:
  207.8 6.1 %copy-start = (f32[1,128,2048]{2,1,0:T(8,128)S(1)}, f32[1,128,2048]{2,1,0:T(8,128)}, u32[]{:S(2)}) copy-start(f32[1,128,2048]{2,1,0:T(8,128)} %module_two.1) | copy-start | bytes 3145732
  207.8 6.1 %copy-start.1 = (f32[1,128,2048]{2,1,0:T(8,128)S(1)}, f32[1,128,2048]{2,1,0:T(8,128)}, u32[]{:S(2)}) copy-start(f32[1,128,2048]{2,1,0:T(8,128)} %param.15) | copy-start | bytes 3145732
  207.8 6.1 %copy-start.2 = (f32[128,2048]{1,0:T(8,128)S(1)}, f32[128,2048]{1,0:T(8,128)}, u32[]{:S(2)}) copy-start(f32[128,2048]{1,0:T(8,128)} %get-tuple-element.7) | copy-start | bytes 3145732

commit v7 on v6

--- a/solution.py
+++ b/solution.py
@@ -228,7 +228,7 @@
 
     def send_slots(m):
         def send(turn, n):
-            t = n * 53 % PATHS
+            t = n * 85 % PATHS
             u = lax.rem(turn * 5 + t // 8, 16)
             to_high = lax.rem(high + lax.rem(u, 2), 2)
             to_z = lax.rem(z + lax.rem(lax.div(u, 2), 4), 4)

time: 216 us -> 215 us (level)
  no operation moved by 1% of the time
where the time goes in v7:
time: 215 us; the launch traced here: 214 us
  Pallas kernels  206 us (96%)
  other arithmetic  7.76 us (4%)
    pallas_call x1, Pallas kernels, one_round(): pl.pallas_call(round_kernel, out_shape=(jax.ShapeDtypeStruct((4, PATHS, 8...  206 us
    sub x1, other arithmetic, shards(): module_one - outer_rate * (outer_moment * next_moment_one + avg_one[None])  6.09 us

profile of v7, /device:TPU:0, one launch (start us, length us, event | category | flops | bytes accessed | tf_op | source)
XLA Modules:
  0.0 214.5 jit_solution(5826106534131949148)
XLA Ops:
  0.6 206.0 %round.1 = (bf16[4,128,8,512]{3,2,1,0:T(8,128)(2,1)}, bf16[4,1024,512]{2,1,0:T(8,128)(2,1)}, f32[256,2048]{1,0:T(8,128)}, f32[128,2048]{1,0:T(8,128)}) custom-call(s32[2,1,128]{2,1,0:T(1,128)} %bitcast.19, s32[8,16]{1,0:T(8,128)} %bitcast.18, bf16[2,128,2048]{2,1,0:T(8,128)(2,1)} %docs.1, bf16[2,128,2048]{2,1,0:T(8,128)(2,1)} %targs.1, ...), custom_call_target="tpu_custom_call" | custom-call | tf_op jit(solution)/shard_map/round/pallas_call | solution.py:534
  206.7 0.0 copy-start
  206.7 0.0 copy-start.1
  206.7 0.0 copy-start.2
  206.7 6.1 %fusion.1 = (f32[1,256,2048]{2,1,0:T(8,128)}, f32[1,256,2048]{2,1,0:T(8,128)}) fusion(f32[1,256,2048]{2,1,0:T(8,128)} %module_one.1, f32[256,2048]{1,0:T(8,128)} %get-tuple-element.6, f32[1,256,2048]{2,1,0:T(8,128)} %param.14), kind=kLoop, calls=%fused_computation.3 | loop fusion | flops 3145728 | bytes 10485760 | tf_op jit(solution)/shard_map/sub | solution.py:566
  212.8 0.0 copy-done
  212.8 0.0 copy-done.1
  212.8 0.0 copy-done.2
  212.8 1.7 fusion.3
Async XLA Ops:
  206.7 6.1 %copy-start = (f32[1,128,2048]{2,1,0:T(8,128)S(1)}, f32[1,128,2048]{2,1,0:T(8,128)}, u32[]{:S(2)}) copy-start(f32[1,128,2048]{2,1,0:T(8,128)} %module_two.1) | copy-start | bytes 3145732
  206.7 6.1 %copy-start.1 = (f32[1,128,2048]{2,1,0:T(8,128)S(1)}, f32[1,128,2048]{2,1,0:T(8,128)}, u32[]{:S(2)}) copy-start(f32[1,128,2048]{2,1,0:T(8,128)} %param.15) | copy-start | bytes 3145732
  206.7 6.1 %copy-start.2 = (f32[128,2048]{1,0:T(8,128)S(1)}, f32[128,2048]{1,0:T(8,128)}, u32[]{:S(2)}) copy-start(f32[128,2048]{1,0:T(8,128)} %get-tuple-element.7) | copy-start | bytes 3145732
